TPU v7x, 256 devices: a whole 4x4x8 slice. The times are simulated.
256 devices in a mesh: row: 32 (over z_lo, x, core), rhs: 8 (over y, z_hi).
Axes of the slice: x: 4, y: 4, z: 8 (z_hi: 2, z_lo: 4; z = z_hi * 4 + z_lo), core: 2. Of those that a mesh axis runs over, the one named last changes fastest.
Arguments:
- rhs_in: float32 [2, 1024, 16384], P(None, ('rhs', 'row')), may hold values from -6 to 6
- pivots: int32 [16384], replicated, may hold values from 0 to 16383, each once
- owners: int32 [32], replicated, may hold values from 0 to 31, each once
- panel_first: float32 [2, 16384, 512], P(None, 'row'), may hold values from -0.1875 to 0.1875
- panel_second: float32 [2, 16384, 512], P(None, 'row'), may hold values from -0.1875 to 0.1875
- inverse_first: float32 [2, 512, 512], replicated, may hold values from -0.1875 to 0.1875
- inverse_second: float32 [2, 512, 512], replicated, may hold values from -0.1875 to 0.1875
Outputs:
- solved_rhs: float32 [2, 1024, 16384], P(None, 'rhs', 'row')
Inputs may be any that keep to these rules, and one draw needn't show every extreme that they name: `pivots`: each row number occurs once. `owners`: each device index along row occurs once.
All inputs are finite; a program needn't handle non-finite values.
Results may differ from a plain program's by a relative error of at most 0.0001.
Values sent between devices are 32-bit elements; how exact they have to be, the bound alone decides.
No kernel may reach another device: no remote copies, remote signals or barrier semaphores. Data moves between devices by JAX's collectives and lax.ppermute only.
A program may use at most 128 MiB of HBM per device.

v0:
```python
import jax
import jax.numpy as jnp
from jax import lax
from jax.sharding import PartitionSpec as P


def broadcast(shard, axis, root):
    mine = lax.axis_index(axis) == root
    return lax.psum(jnp.where(mine, shard, jnp.zeros_like(shard)), axis)


def complex_product(operand, matrix):
    contract = (((1,), (1,)), ((), ()))

    def multiply(first, second):
        return lax.dot_general(
            first,
            second,
            contract,
            precision=lax.Precision.HIGHEST,
            preferred_element_type=jnp.float32,
        )

    real_part = multiply(operand[0], matrix[0]) - multiply(operand[1], matrix[1])
    imag_part = multiply(operand[0], matrix[1]) + multiply(operand[1], matrix[0])
    return jnp.stack([real_part, imag_part])


def shards(rhs_in, pivots, owners, panel_first, panel_second, inverse_first, inverse_second):
    blocks = owners.shape[0]
    block_size = panel_first.shape[2]
    slot_block = jnp.zeros((blocks,), jnp.int32).at[owners].set(jnp.arange(blocks, dtype=jnp.int32))
    row_index = (
        slot_block[:, None] * block_size + jnp.arange(block_size, dtype=jnp.int32)[None, :]
    ).reshape(-1)
    ordered = jnp.take(rhs_in, jnp.take(pivots, row_index), axis=2)
    my_index = lax.axis_index("row")
    my_block = slot_block[my_index]
    current = lax.all_to_all(ordered, "row", split_axis=2, concat_axis=1, tiled=True)
    sections = ((panel_first, inverse_first), (panel_second, inverse_second))
    for block_step in range(2):
        panel_rows, inverse = sections[block_step]
        holder = owners[block_step]
        solved = complex_product(current, inverse)
        solution = broadcast(solved, "row", holder)
        update = complex_product(solution, panel_rows)
        current = jnp.where(my_block > block_step, current - update, current)
        current = jnp.where(my_block == block_step, solution, current)
    return current


def solution(mesh):
    return jax.shard_map(
        shards,
        mesh=mesh,
        in_specs=(
            P(None, ("rhs", "row"), None),
            P(),
            P(),
            P(None, "row", None),
            P(None, "row", None),
            P(),
            P(),
        ),
        out_specs=P(None, "rhs", "row"),
        check_vma=False,
    )
```

profile of v0, /device:TPU:1, one launch (start us, length us, event | category | flops | bytes accessed | tf_op | source)
XLA Modules:
  0.0 983.9 jit_solution(494485509080680540)
XLA Ops:
  6.5 0.7 compare_select_fusion.4
  7.2 0.7 scatter_custom_fusion
  7.9 0.1 fusion.51
  8.0 0.1 copy.12
  8.1 0.1 compare_select_fusion.1
  8.2 90.5 %gather_fusion = s32[16384]{0:T(1024)S(1)} fusion(s32[16384]{0:T(1024)S(1)} %copy-done, s32[16384]{0:T(1024)S(1)} %broadcast_clamp_fusion.1), kind=kCustom, calls=%fused_computation | custom fusion | bytes 196608 | tf_op jit(solution)/shard_map/jit(_take)/gather | solution.py:36
  98.8 0.2 compare_select_fusion
  99.0 14.8 %copy.9 = f32[2,4,16384]{1,0,2:T(2,128)} copy(f32[2,4,16384]{2,1,0:T(4,128)S(1)} %copy-done.8) | data formatting | bytes 1048576 | tf_op args[0]
  113.9 118.1 %gather_fusion.1 = f32[16384,2,4]{2,1,0:T(2,128)} fusion(f32[2,4,16384]{1,0,2:T(2,128)} %copy.9, s32[16384]{0:T(1024)S(1)} %broadcast_clamp_fusion), kind=kCustom, calls=%fused_computation.1 | custom fusion | bytes 1114112 | tf_op jit(solution)/shard_map/jit(_take)/gather | solution.py:36
  231.9 59.0 %fusion.56 = f32[16384,2,4]{2,1,0:T(2,128)} fusion(f32[16384,2,4]{2,1,0:T(2,128)} %gather_fusion.1, pred[16384]{0:T(1024)(128)(4,1)S(1)} %compare_and_fusion), kind=kLoop, calls=%fused_computation.89 | loop fusion | flops 131072 | bytes 1064960
  290.9 27.6 %reshape.122 = f32[32,1,4096]{2,1,0:T(1,128)} reshape(f32[16384,2,4]{2,1,0:T(2,128)} %fusion.56) | data formatting | bytes 1048576
  318.6 10.0 %all-to-all-start = ((f32[32,1,4096]{2,1,0:T(1,128)}), f32[32,1,4096]{2,1,0:T(1,128)S(1)}, u32[]{:S(2)}, u32[]{:S(2)}) async-start(f32[32,1,4096]{2,1,0:T(1,128)} %reshape.122), calls=%async_computation | async-start | bytes 1048576 | tf_op jit(solution)/shard_map/all_to_all | solution.py:39
  328.6 0.2 all-reduce.3.cloned.1.call-start
  328.8 0.6 fusion.55
  330.1 14.9 %all-to-all-done = f32[32,1,4096]{2,1,0:T(1,128)S(1)} async-done(((f32[32,1,4096]{2,1,0:T(1,128)}), f32[32,1,4096]{2,1,0:T(1,128)S(1)}, u32[]{:S(2)}, u32[]{:S(2)}) %all-to-all-start) | async-done | bytes 524320 | tf_op jit(solution)/shard_map/all_to_all | solution.py:39
  345.0 0.5 broadcast.121
  345.5 1.9 reduce
  347.4 27.8 %reshape.123 = f32[16384,2,4]{2,1,0:T(2,128)} reshape(f32[32,4096]{1,0:T(8,128)S(1)} %reduce) | data formatting | bytes 1048576
  375.3 19.1 %copy.10 = f32[2,4,32,512]{3,1,2,0:T(4,128)S(1)} copy(f32[2,4,32,512]{1,0,3,2:T(2,128)} %bitcast.111) | data formatting | bytes 1048576 | tf_op jit(solution)/shard_map/all_to_all | solution.py:39
  394.4 0.7 fusion.54
  395.1 0.1 squeeze.73
  395.2 1.2 fusion.26
  396.4 1.2 fusion.30
  397.6 1.0 squeeze.75
  398.6 1.2 fusion.7
  399.8 1.2 fusion.6
  401.0 0.8 maximum_select_fusion
  401.9 0.3 all-reduce.5.cloned.1.call-start
  402.2 0.6 dynamic_slice.3
  404.5 0.2 all_to_all.16
  404.7 274.4 %all-reduce.3.cloned.1.call-done = f32[2,128,512]{2,1,0:T(8,128)} async-done(((f32[2,128,512]{2,1,0:T(8,128)}), f32[2,128,512]{2,1,0:T(8,128)}) %all-reduce.3.cloned.1.call-update) | async-done | bytes 524304 | tf_op jit(solution)/shard_map/psum | solution.py:9
  679.1 2.2 fusion.20
  681.3 2.1 fusion.24
  683.4 1.2 fusion.4
  684.6 1.2 fusion.5
  685.8 0.2 fusion.48
  686.0 0.2 copy-done.4
  686.2 1.2 fusion.14
  687.4 1.2 fusion.18
  688.6 1.2 fusion.2
  689.8 1.2 fusion.3
  691.0 0.8 maximum_select_fusion.1
  693.0 276.4 %all-reduce.5.cloned.1.call-done = f32[2,128,512]{2,1,0:T(8,128)} async-done(((f32[2,128,512]{2,1,0:T(8,128)}), f32[2,128,512]{2,1,0:T(8,128)}) %all-reduce.5.cloned.1.call-update) | async-done | bytes 524304 | tf_op jit(solution)/shard_map/psum | solution.py:9
  969.4 2.2 fusion.8
  971.6 2.1 fusion.12
  973.8 1.2 fusion
  975.0 1.2 fusion.1
  976.1 1.0 fusion.49
  (27 shorter events, 0.2 us)
Async XLA Ops:
  6.5 1.7 copy-start
  8.2 90.8 %copy-start.8 = (f32[2,4,16384]{2,1,0:T(4,128)S(1)}, f32[2,4,16384]{2,1,0:T(4,128)}, u32[]{:S(2)}) copy-start(f32[2,4,16384]{2,1,0:T(4,128)} %param.7) | copy-start | bytes 1572868
  290.9 37.9 %copy-start.9 = (s32[32]{0:T(128)S(1)}, s32[32]{0:T(128)}, u32[]{:S(2)}) copy-start(s32[32]{0:T(128)} %param.9) | copy-start | bytes 388
  318.6 26.4 %all-to-all-start = ((f32[32,1,4096]{2,1,0:T(1,128)}), f32[32,1,4096]{2,1,0:T(1,128)S(1)}, u32[]{:S(2)}, u32[]{:S(2)}) async-start(f32[32,1,4096]{2,1,0:T(1,128)} %reshape.122), calls=%async_computation | async-start | bytes 1048576 | tf_op jit(solution)/shard_map/all_to_all | solution.py:39
  328.6 350.5 %all-reduce.3.cloned.1.call-start = ((), (), s32[]{:S(2)}) async-start(), calls=%async_computation.1 | async-start | bytes 1048576 | tf_op jit(solution)/shard_map/psum | solution.py:9
  375.3 20.0 %copy-start.2 = (f32[2,512,512]{2,1,0:T(8,128)S(1)}, f32[2,512,512]{2,1,0:T(8,128)}, u32[]{:S(2)}) copy-start(f32[2,512,512]{2,1,0:T(8,128)} %param.12) | copy-start | bytes 6291460
  401.0 278.1 %copy-start.3 = (f32[2,512,512]{2,1,0:T(8,128)S(1)}, f32[2,512,512]{2,1,0:T(8,128)}, u32[]{:S(2)}) copy-start(f32[2,512,512]{2,1,0:T(8,128)} %param.10) | copy-start | bytes 6291460
  401.9 567.5 %all-reduce.5.cloned.1.call-start = ((), (), s32[]{:S(2)}) async-start(), calls=%async_computation.2 | async-start | bytes 1048576 | tf_op jit(solution)/shard_map/psum | solution.py:9
  679.1 4.3 copy-start.6
  684.6 1.6 copy-start.4
  689.8 279.7 %copy-start.5 = (f32[2,512,512]{2,1,0:T(8,128)S(1)}, f32[2,512,512]{2,1,0:T(8,128)}, u32[]{:S(2)}) copy-start(f32[2,512,512]{2,1,0:T(8,128)} %param.11) | copy-start | bytes 6291460
  969.4 4.3 copy-start.7
  973.8 3.3 copy-start.1
Sparse Core Ops, SparseCore 0:
  402.0 277.0 all-reduce.2
  691.9 277.4 all-reduce.4
where the time goes:
time: 985 us; the launch traced here: 984 us
  waiting for transfers between devices  566 us (57%)
  local copies, waits for them, and re-layouts  303 us (31%)
  other arithmetic  64.8 us (7%)
  matrix products  22.7 us (2%)
  between operations  17.3 us (2%)
  starting transfers between devices  10.5 us (1%)
    psum x2, waiting for transfers between devices, broadcast(): return lax.psum(jnp.where(mine, shard, jnp.zeros_like(shard)), axis)  551 us
    gather x2, local copies, waits for them, and re-layouts, shards(): ordered = jnp.take(rhs_in, jnp.take(pivots, row_index), axis=2)  209 us
    unnamed x25, local copies, waits for them, and re-layouts  70.7 us
    unnamed x2, other arithmetic  59.1 us
    dot_general x16, matrix products, multiply(): lax.dot_general(first, second, contract, precision=lax.Precision.HIGHEST,...  22.7 us
    all_to_all x3, local copies, waits for them, and re-layouts, shards(): lax.all_to_all(ordered, 'row', split_axis=2, concat_axis=1, tiled=True)  19.8 us
  transfers between devices with their start and end apart: 3, of which 3 were waited for; matrix products, arithmetic and copies ran while one was open for 0% of the time, Pallas kernels for 0%

commit v1 on v0

v1 whole, which is shorter than its diff:
```python
import functools

import jax
import jax.numpy as jnp
from jax import lax
from jax.experimental import pallas as pl
from jax.experimental.pallas import tpu as pltpu
from jax.sharding import Mesh, PartitionSpec as P

F32 = jnp.float32
BF16 = jnp.bfloat16
NT = (((1,), (1,)), ((), ()))
NN = (((1,), (0,)), ((), ()))


def split(v):
    high = v.astype(BF16)
    return high, (v - high.astype(F32)).astype(BF16)


def turned(v):
    tiles = v.reshape(v.shape[0] // 8, 8, v.shape[1])
    row = lax.broadcasted_iota(jnp.int32, tiles.shape, 1)
    swapped = pltpu.roll(tiles, 4, 1)
    return jnp.where(row < 4, -swapped, swapped).reshape(v.shape)


def dot(a, b, dims=NT):
    return lax.dot_general(a, b, dims, preferred_element_type=F32)


def gather_columns(left, pivots):
    n = pivots.shape[1]
    major = pivots >> 7
    minor = pivots & 127
    pick = (lax.broadcasted_iota(jnp.int32, (128, n), 0) == major).astype(F32).astype(BF16)
    product = dot(left, jnp.concatenate([pick, pick], 0), NN).reshape(8, 16, 8, n)
    row = lax.broadcasted_iota(jnp.int32, (8, n), 0)
    found = jnp.zeros((8, 8, n), F32)
    for j in range(16):
        found = jnp.where((row + 8 * j == minor)[None], product[:, j], found)
    return found.sum(axis=1)


def pieces_kernel(place_ref, panel_ref, out_ref):
    half = place_ref[1]
    for z in range(4):
        for k in range(8):
            start = pl.multiple_of(64 * k + 16 * z + 8 * half, 8)
            for part in range(2):
                out_ref[z * 8 + k, part] = panel_ref[part, pl.ds(start, 8), :]


def make_pieces(place, panel):
    return pl.pallas_call(
        pieces_kernel,
        grid_spec=pltpu.PrefetchScalarGridSpec(
            num_scalar_prefetch=1,
            grid=(1,),
            in_specs=[pl.BlockSpec((2, 512, 128), lambda i, place: (0, 0, place[0]))],
            out_specs=pl.BlockSpec((32, 2, 8, 128), lambda i, place: (0, 0, 0, 0)),
        ),
        out_shape=jax.ShapeDtypeStruct((32, 2, 8, 128), F32),
        name="pieces",
    )(place, panel)


def head_kernel(rhs_ref, pivots_ref, inverse_ref, left_ref, out_ref):
    for part in range(2):
        for c in range(4):
            r = part * 4 + c
            high, low = split(rhs_ref[part, :, c, :].T)
            left_ref[pl.ds(128 * r, 128), 0:128] = high
            left_ref[pl.ds(128 * r, 128), 128:256] = low
    left = left_ref[...]
    first = [gather_columns(left, pivots_ref[0:1, 256 * k : 256 * k + 256]) for k in range(2)]
    second = [gather_columns(left, pivots_ref[1:2, 256 * k : 256 * k + 256]) for k in range(2)]
    first = jnp.concatenate(first, 1)
    operand = jnp.concatenate([first, turned(first)], 1)
    high, low = split(operand)
    w_high, w_low = split(jnp.concatenate([inverse_ref[0], inverse_ref[1]], 1))
    both = dot(jnp.concatenate([high, low], 0), w_high)
    solved = both[0:8] + both[8:16] + dot(high, w_low)
    second = jnp.concatenate(second, 1)
    for k in range(4):
        out_ref[k, 0] = solved
        out_ref[k, 1] = second


def head(rhs, pivots, inverse):
    return pl.pallas_call(
        head_kernel,
        grid=(1,),
        in_specs=[
            pl.BlockSpec((2, 128, 4, 128), lambda i: (0, 0, 0, 0)),
            pl.BlockSpec((8, 512), lambda i: (0, 0)),
            pl.BlockSpec((2, 512, 512), lambda i: (0, 0, 0)),
        ],
        out_specs=[
            pl.BlockSpec((1024, 256), lambda i: (0, 0)),
            pl.BlockSpec((4, 2, 8, 512), lambda i: (0, 0, 0, 0)),
        ],
        out_shape=[
            jax.ShapeDtypeStruct((1024, 256), BF16),
            jax.ShapeDtypeStruct((4, 2, 8, 512), F32),
        ],
        name="head",
    )(rhs, pivots, inverse)


def gather_kernel(owners_ref, left_ref, pivots_ref, *rest):
    out_ref = rest[-1]
    left = left_ref[...]
    for k in range(2):
        out_ref[0, :, 256 * k : 256 * k + 256] = gather_columns(left, pivots_ref[0, :, 256 * k : 256 * k + 256])


def gather(owners, left, pivots, start, count, into=None):
    specs = [
        pl.BlockSpec((1024, 256), lambda i, owners: (0, 0)),
        pl.BlockSpec((1, 1, 512), lambda i, owners: (i + start, 0, 0)),
    ]
    operands = [owners, left, pivots]
    aliases = {}
    if into is not None:
        specs.append(pl.BlockSpec(memory_space=pl.ANY))
        operands.append(into)
        aliases = {3: 0}
    return pl.pallas_call(
        gather_kernel,
        grid_spec=pltpu.PrefetchScalarGridSpec(
            num_scalar_prefetch=1,
            grid=(count,),
            in_specs=specs,
            out_specs=pl.BlockSpec((1, 8, 512), lambda i, owners: (owners[i + start], 0, 0)),
        ),
        out_shape=jax.ShapeDtypeStruct((32, 8, 512), F32),
        input_output_aliases=aliases,
        name="gather_blocks",
    )(*operands)


def operands_kernel(all_ref, high_ref, low_ref):
    for k in range(0, 32, 2):
        a, b = k // 16, (k // 4) % 4
        z = k % 4
        v = jnp.concatenate([all_ref[a, b, z, 0], all_ref[a, b, z + 1, 0]], 0)
        high, low = split(jnp.concatenate([v, turned(v)], 1))
        high_ref[pl.ds(8 * k, 16), :] = high
        low_ref[pl.ds(8 * k, 16), :] = low


def make_operands(gathered):
    return pl.pallas_call(
        operands_kernel,
        grid=(1,),
        in_specs=[pl.BlockSpec((2, 4, 4, 1, 8, 512), lambda i: (0, 0, 0, 0, 0, 0))],
        out_specs=[pl.BlockSpec((256, 1024), lambda i: (0, 0))] * 2,
        out_shape=[jax.ShapeDtypeStruct((256, 1024), BF16)] * 2,
        name="operands",
    )(gathered)


def cross_kernel(pieces_ref, high_ref, low_ref, out_ref, panel_ref):
    for z in range(4):
        for r in range(8):
            o, cb = 2 * z + r // 4, r % 4
            for part in range(2):
                panel_ref[pl.ds(8 * o, 8), pl.ds(512 * part + 128 * cb, 128)] = pieces_ref[z * 8 + r, part]
    q_high, q_low = split(panel_ref[...])
    both = dot(jnp.concatenate([q_high, q_low], 0), high_ref[...])
    value = both[0:64] + both[64:128] + dot(q_high, low_ref[...])
    for k in range(8):
        out_ref[k] = value


def cross(pieces, high, low):
    return pl.pallas_call(
        cross_kernel,
        out_shape=jax.ShapeDtypeStruct((8, 64, 256), F32),
        scratch_shapes=[pltpu.VMEM((64, 1024), F32)],
        name="cross",
    )(pieces, high, low)


def weights(ref):
    return split(jnp.concatenate([ref[0], ref[1]], 1))


def triple(high, low, w_high, w_low):
    return dot(high, w_high) + (dot(low, w_high) + dot(high, w_low))


def base_kernel(block_ref, current_ref, gathered_ref, high_ref, low_ref, panel_ref, out_ref):
    block = block_ref[0]
    w_high, w_low = weights(panel_ref)
    update = triple(high_ref[...], low_ref[...], w_high, w_low)
    for k in range(32):
        a, b, z = k // 16, (k // 4) % 4, k % 4
        d = z * 8 + b * 2 + a
        later = current_ref[d] - update[8 * k : 8 * k + 8]
        out_ref[pl.ds(8 * k, 8), :] = jnp.where(block == 0, gathered_ref[a, b, z, 0], later)


def make_base(block, current, gathered, high, low, panel):
    vmem = pl.BlockSpec(memory_space=pltpu.VMEM)
    return pl.pallas_call(
        base_kernel,
        in_specs=[pl.BlockSpec(memory_space=pltpu.SMEM)] + [vmem] * 5,
        out_shape=jax.ShapeDtypeStruct((256, 512), F32),
        name="base",
    )(block, current, gathered, high, low, panel)


def tail_kernel(block_ref, base_ref, gathered_ref, cross_ref, inverse_ref, panel_ref, out_ref):
    block = block_ref[0]
    other = jnp.concatenate([gathered_ref[k // 16, (k // 4) % 4, k % 4, 1] for k in range(32)], 0)
    value = other - cross_ref[...].reshape(512, 256).T
    high, low = split(jnp.concatenate([value, turned(value)], 1))
    solved = triple(high, low, *weights(inverse_ref))
    high, low = split(jnp.concatenate([solved, turned(solved)], 1))
    update = triple(high, low, *weights(panel_ref))
    base = base_ref[...]
    result = jnp.where(block > 1, base - update, jnp.where(block == 1, solved, base))
    for k in range(32):
        a, b, z = k // 16, (k // 4) % 4, k % 4
        d = z * 8 + b * 2 + a
        out_ref[0, pl.ds(4 * d, 4), :] = result[8 * k : 8 * k + 4]
        out_ref[1, pl.ds(4 * d, 4), :] = result[8 * k + 4 : 8 * k + 8]


def tail(block, base, gathered, crossed, inverse, panel):
    vmem = pl.BlockSpec(memory_space=pltpu.VMEM)
    return pl.pallas_call(
        tail_kernel,
        in_specs=[pl.BlockSpec(memory_space=pltpu.SMEM)] + [vmem] * 5,
        out_shape=jax.ShapeDtypeStruct((2, 128, 512), F32),
        name="tail",
    )(block, base, gathered, crossed, inverse, panel)


def exchange(v, axis):
    return lax.all_to_all(v, axis, 0, 0, tiled=True)


def repeat(v, n):
    return jnp.broadcast_to(v[None], (n,) + v.shape)


def shards(rhs_in, pivots, owners, panel_first, panel_second, inverse_first, inverse_second):
    row = ("z", "x", "c")
    me = lax.axis_index(row)
    replica = lax.axis_index("rhs")
    block = jnp.sum(jnp.where(owners == me, jnp.arange(32, dtype=jnp.int32), 0)).reshape(1)
    place = jnp.stack([replica & 3, replica >> 2]).astype(jnp.int32)
    rhs = rhs_in.reshape(2, 4, 128, 128).transpose(0, 2, 1, 3)
    piv = pivots.reshape(32, 512)

    pieces = exchange(make_pieces(place, panel_first), row)
    left, mine = head(rhs, piv, inverse_first)
    gathered = exchange(mine, "z")
    piece = lax.dynamic_index_in_dim(pieces, owners[1], 0, keepdims=False)
    pieces = exchange(repeat(piece, 32), ("z", "rhs"))
    gathered = exchange(repeat(gathered, 4), "x")
    blocks = gather(owners, left, piv.reshape(32, 1, 512), 2, 15)
    gathered = exchange(repeat(gathered, 2), "c")
    blocks = gather(owners, left, piv.reshape(32, 1, 512), 17, 15, blocks)
    current = exchange(blocks, row)
    high, low = make_operands(gathered)
    crossed = exchange(cross(pieces, high, low), ("x", "c"))
    base = make_base(block, current, gathered, high, low, panel_first)
    return tail(block, base, gathered, crossed, inverse_second, panel_second)


def solution(mesh):
    fine = Mesh(mesh.devices.reshape(4, 4, 2, 8), ("z", "x", "c", "rhs"))
    row = ("z", "x", "c")
    return jax.shard_map(
        shards,
        mesh=fine,
        in_specs=(
            P(None, ("rhs",) + row, None),
            P(),
            P(),
            P(None, row, None),
            P(None, row, None),
            P(),
            P(),
        ),
        out_specs=P(None, "rhs", row),
        check_vma=False,
    )
```

time: 985 us -> 131 us (0.13)
  waiting for transfers between devices: 566 us -> 23.9 us
  local copies, waits for them, and re-layouts: 303 us -> 4.54 us
  other arithmetic: 64.8 us -> 1.26 us
  Pallas kernels: 0 us -> 44.2 us
  blocking collectives: 0 us -> 24.8 us
  matrix products: 22.7 us -> 0 us
  starting transfers between devices: 10.5 us -> 28.5 us
  between operations: 17.3 us -> 1.74 us
    psum x2 -> x0, waiting for transfers between devices: 551 us -> none  [broadcast(): return lax.psum(jnp.where(mine, shard, jnp.zeros_like(shard)), axis)]
    gather x2 -> x0, local copies, waits for them, and re-layouts: 209 us -> none  [shards(): ordered = jnp.take(rhs_in, jnp.take(pivots, row_index), axis=2)]
    unnamed x25 -> x10, local copies, waits for them, and re-layouts: 70.7 us -> 0.82 us
    unnamed x2 -> x0, other arithmetic: 59.1 us -> none
    pallas_call x0 -> x8, Pallas kernels: none -> 44.2 us  [the longest x2 21.7 us: gather(): pl.pallas_call(gather_kernel, grid_spec=pltpu.PrefetchScalarGridSpec(num_...]
    all_to_all x0 -> x2, blocking collectives: none -> 24.8 us  [exchange(): return lax.all_to_all(v, axis, 0, 0, tiled=True)]
    dot_general x16 -> x0, matrix products: 22.7 us -> none  [multiply(): lax.dot_general(first, second, contract, precision=lax.Precision.HIGHEST,...]
    all_to_all x3 -> x0, local copies, waits for them, and re-layouts: 19.8 us -> none  [shards(): lax.all_to_all(ordered, 'row', split_axis=2, concat_axis=1, tiled=True)]
  transfers between devices with their start and end apart: 3 -> 5, of which waited for: 3 -> 4; matrix products, arithmetic and copies ran while one was open for 0% -> 1% of each run, Pallas kernels for 0% -> 26%
where the time goes in v1:
time: 131 us; the launch traced here: 129 us
  Pallas kernels  44.2 us (34%)
  starting transfers between devices  28.5 us (22%)
  blocking collectives  24.8 us (19%)
  waiting for transfers between devices  23.9 us (18%)
  local copies, waits for them, and re-layouts  4.54 us (3%)
  between operations  1.74 us (1%)
    all_to_all x5, starting transfers between devices, exchange(): return lax.all_to_all(v, axis, 0, 0, tiled=True)  28.5 us
    all_to_all x2, blocking collectives, exchange(): return lax.all_to_all(v, axis, 0, 0, tiled=True)  24.8 us
    all_to_all x5, waiting for transfers between devices, exchange(): return lax.all_to_all(v, axis, 0, 0, tiled=True)  23.9 us
    pallas_call x2, Pallas kernels, gather(): pl.pallas_call(gather_kernel, grid_spec=pltpu.PrefetchScalarGridSpec(num_...  21.7 us
    pallas_call x1, Pallas kernels, tail(): pl.pallas_call(tail_kernel, in_specs=[pl.BlockSpec(memory_space=pltpu.SME...  6.31 us
    pallas_call x1, Pallas kernels, make_base(): pl.pallas_call(base_kernel, in_specs=[pl.BlockSpec(memory_space=pltpu.SME...  4.87 us
    pallas_call x1, Pallas kernels, head(): pl.pallas_call(head_kernel, grid=(1,), in_specs=[pl.BlockSpec((2, 128, 4,...  4 us
  transfers between devices with their start and end apart: 5, of which 4 were waited for; matrix products, arithmetic and copies ran while one was open for 1% of the time, Pallas kernels for 26%

profile of v1, /device:TPU:1, one launch (start us, length us, event | category | flops | bytes accessed | tf_op | source)
XLA Modules:
  0.0 128.9 jit_solution(9153565340821228584)
XLA Ops:
  0.0 1.5 %reshape.13.pivots_ref = s32[32,512]{1,0:T(8,128)} reshape(s32[16384]{0:T(1024)} %param.8) | data formatting | bytes 131072 | tf_op jit(solution)/shard_map/reshape | solution.py:257
  1.5 4.0 %head.1 = (bf16[1024,256]{1,0:T(8,128)(2,1)}, f32[4,2,8,512]{3,2,1,0:T(8,128)}) custom-call(f32[2,128,4,128]{3,2,1,0:T(4,128)} %bitcast.12, s32[32,512]{1,0:T(8,128)} %reshape.13.pivots_ref, f32[2,512,512]{2,1,0:T(8,128)} %inverse_ref.2), custom_call_target="tpu_custom_call" | custom-call | tf_op jit(solution)/shard_map/head/pallas_call | solution.py:91
  5.5 6.4 %all-to-all-start.1 = ((f32[4,2,8,512]{3,2,1,0:T(8,128)}), f32[4,2,8,512]{3,2,1,0:T(8,128)S(1)}, u32[]{:S(2)}, u32[]{:S(2)}) async-start(f32[4,2,8,512]{3,2,1,0:T(8,128)} %get-tuple-element.10), calls=%async_computation.1 | async-start | bytes 262144 | tf_op jit(solution)/shard_map/all_to_all | solution.py:243
  11.9 0.6 pad_add_fusion.place_ref
  12.5 0.0 copy-start.3
  12.5 2.6 %pieces.1 = f32[32,2,8,128]{3,2,1,0:T(8,128)} custom-call(s32[2]{0:T(128)} %pad_add_fusion.place_ref, f32[2,512,512]{2,1,0:T(8,128)} %panel_ref.4), custom_call_target="tpu_custom_call" | custom-call | tf_op jit(solution)/shard_map/pieces/pallas_call | solution.py:55
  15.0 1.6 %all-to-all-done.1 = f32[4,2,8,512]{3,2,1,0:T(8,128)S(1)} async-done(((f32[4,2,8,512]{3,2,1,0:T(8,128)}), f32[4,2,8,512]{3,2,1,0:T(8,128)S(1)}, u32[]{:S(2)}, u32[]{:S(2)}) %all-to-all-start.1) | async-done | bytes 131104 | tf_op jit(solution)/shard_map/all_to_all | solution.py:243
  16.7 18.7 %all_to_all.35 = f32[32,2,8,128]{3,2,1,0:T(8,128)S(1)} all-to-all(f32[32,2,8,128]{3,2,1,0:T(8,128)} %pieces.1), channel_id=1, replica_groups=mesh['z'=4,'x'=4,'c'=2,'rhs'=8] {'z','x','c'}, dimensions={0} | all-to-all | bytes 524288 | tf_op jit(solution)/shard_map/all_to_all | solution.py:243
  35.3 0.9 broadcast_in_dim.13
  36.2 3.5 %all-to-all-start.2 = ((f32[4,4,2,8,512]{4,3,2,1,0:T(8,128)}), f32[4,4,2,8,512]{4,3,2,1,0:T(8,128)S(1)}, u32[]{:S(2)}, u32[]{:S(2)}) async-start(f32[4,4,2,8,512]{4,3,2,1,0:T(8,128)} %broadcast_in_dim.13), calls=%async_computation.2 | async-start | bytes 1048576 | tf_op jit(solution)/shard_map/all_to_all | solution.py:243
  39.7 0.0 copy-done.3
  39.7 0.6 slice.3
  41.9 7.1 %all-to-all-done.2 = f32[4,4,2,8,512]{4,3,2,1,0:T(8,128)S(1)} async-done(((f32[4,4,2,8,512]{4,3,2,1,0:T(8,128)}), f32[4,4,2,8,512]{4,3,2,1,0:T(8,128)S(1)}, u32[]{:S(2)}, u32[]{:S(2)}) %all-to-all-start.2) | async-done | bytes 524320 | tf_op jit(solution)/shard_map/all_to_all | solution.py:243
  49.0 0.1 broadcast_in_dim.26
  49.1 6.1 %all_to_all.36.all_ref.gathered_ref = f32[2,4,4,2,8,512]{5,4,3,2,1,0:T(8,128)} all-to-all(f32[2,4,4,2,8,512]{5,4,3,2,1,0:T(8,128)S(1)} %broadcast_in_dim.26), channel_id=1, replica_groups=mesh['z'=4,'x'=4,'c'=2,'rhs'=8] {'c'}, dimensions={0} | all-to-all | bytes 2097152 | tf_op jit(solution)/shard_map/all_to_all | solution.py:243
  55.2 0.7 broadcast_in_dim.28
  55.9 8.9 %all-to-all-start.5 = ((f32[32,2,8,128]{3,2,1,0:T(8,128)}), f32[32,2,8,128]{3,2,1,0:T(8,128)S(1)}, u32[]{:S(2)}, u32[]{:S(2)}) async-start(f32[32,2,8,128]{3,2,1,0:T(8,128)} %broadcast_in_dim.28), calls=%async_computation.5 | async-start | bytes 524288 | tf_op jit(solution)/shard_map/all_to_all | solution.py:243
  64.8 10.9 %gather_blocks.2.rest_0_ = f32[32,8,512]{2,1,0:T(8,128)} custom-call(s32[32]{0:T(128)} %owners_ref.3, bf16[1024,256]{1,0:T(8,128)(2,1)} %get-tuple-element.9.left_ref, s32[32,1,512]{2,1,0:T(1,128)} %bitcast.10), custom_call_target="tpu_custom_call" | custom-call | tf_op jit(solution)/shard_map/gather_blocks/pallas_call | solution.py:129
  75.7 10.9 %gather_blocks.3 = f32[32,8,512]{2,1,0:T(8,128)} custom-call(s32[32]{0:T(128)} %owners_ref.3, bf16[1024,256]{1,0:T(8,128)(2,1)} %get-tuple-element.9.left_ref, s32[32,1,512]{2,1,0:T(1,128)} %bitcast.11, f32[32,8,512]{2,1,0:T(8,128)} %gather_blocks.2.rest_0_), custom_call_target="tpu_custom_call", output_to_operand_aliasing={{}: (3, {})} | custom-call | tf_op jit(solution)/shard_map/gather_blocks/pallas_call | solution.py:129
  86.5 0.0 all-to-all-done.5.pieces_ref
  86.5 0.0 copy-start.2
  86.5 6.3 %all-to-all-start = ((f32[32,8,512]{2,1,0:T(8,128)}), f32[32,8,512]{2,1,0:T(8,128)S(1)}, u32[]{:S(2)}, u32[]{:S(2)}) async-start(f32[32,8,512]{2,1,0:T(8,128)} %gather_blocks.3), calls=%async_computation | async-start | bytes 1048576 | tf_op jit(solution)/shard_map/all_to_all | solution.py:243
  92.9 0.0 copy-start.4
  92.9 2.2 %operands.1 = (bf16[256,1024]{1,0:T(8,128)(2,1)}, bf16[256,1024]{1,0:T(8,128)(2,1)}) custom-call(f32[2,4,4,2,8,512]{5,4,3,2,1,0:T(8,128)} %all_to_all.36.all_ref.gathered_ref), custom_call_target="tpu_custom_call" | custom-call | tf_op jit(solution)/shard_map/operands/pallas_call | solution.py:154
  95.1 0.0 copy-done.2
  95.1 2.6 %cross.1 = f32[8,64,256]{2,1,0:T(8,128)} custom-call(f32[32,2,8,128]{3,2,1,0:T(8,128)} %copy-done.2, bf16[256,1024]{1,0:T(8,128)(2,1)} %get-tuple-element.11.high_ref, bf16[256,1024]{1,0:T(8,128)(2,1)} %get-tuple-element.12.low_ref), custom_call_target="tpu_custom_call" | custom-call | tf_op jit(solution)/shard_map/cross/pallas_call | solution.py:178
  97.6 11.7 %all-to-all-done.current_ref = f32[32,8,512]{2,1,0:T(8,128)S(1)} async-done(((f32[32,8,512]{2,1,0:T(8,128)}), f32[32,8,512]{2,1,0:T(8,128)S(1)}, u32[]{:S(2)}, u32[]{:S(2)}) %all-to-all-start) | async-done | bytes 524320 | tf_op jit(solution)/shard_map/all_to_all | solution.py:243
  109.3 0.0 copy-start
  109.3 3.4 %all-to-all-start.6 = ((f32[8,64,256]{2,1,0:T(8,128)}), f32[8,64,256]{2,1,0:T(8,128)S(1)}, u32[]{:S(2)}, u32[]{:S(2)}) async-start(f32[8,64,256]{2,1,0:T(8,128)} %cross.1), calls=%async_computation.6 | async-start | bytes 1048576 | tf_op jit(solution)/shard_map/all_to_all | solution.py:243
  112.8 0.0 copy-done.4
  112.8 0.7 fusion
  113.5 0.0 copy-done
  113.5 4.9 %base.1.base_ref = f32[256,512]{1,0:T(8,128)} custom-call(s32[1]{0:T(128)} %bitcast.block_ref, f32[32,8,512]{2,1,0:T(8,128)} %copy-done, f32[2,4,4,2,8,512]{5,4,3,2,1,0:T(8,128)} %all_to_all.36.all_ref.gathered_ref, bf16[256,1024]{1,0:T(8,128)(2,1)} %get-tuple-element.11.high_ref, bf16[256,1024]{1,0:T(8,128)(2,1)} %get-tuple-element.12.low_ref, ...), custom_call_target="tpu_custom_call" | custom-call | tf_op jit(solution)/shard_map/base/pallas_call | solution.py:207
  118.3 3.5 %all-to-all-done.6.cross_ref = f32[8,64,256]{2,1,0:T(8,128)S(1)} async-done(((f32[8,64,256]{2,1,0:T(8,128)}), f32[8,64,256]{2,1,0:T(8,128)S(1)}, u32[]{:S(2)}, u32[]{:S(2)}) %all-to-all-start.6) | async-done | bytes 524320 | tf_op jit(solution)/shard_map/all_to_all | solution.py:243
  121.8 0.0 copy-start.1
  121.8 0.8 copy-done.1
  122.6 6.3 %tail.1 = f32[2,128,512]{2,1,0:T(8,128)} custom-call(s32[1]{0:T(128)} %bitcast.block_ref, f32[256,512]{1,0:T(8,128)} %base.1.base_ref, f32[2,4,4,2,8,512]{5,4,3,2,1,0:T(8,128)} %all_to_all.36.all_ref.gathered_ref, f32[8,64,256]{2,1,0:T(8,128)} %copy-done.1, f32[2,512,512]{2,1,0:T(8,128)} %inverse_ref.3, f32[2,512,512]{2,1,0:T(8,128)} %panel_ref.5), custom_call_target="tpu_custom_call" | custom-call | tf_op jit(solution)/shard_map/tail/pallas_call | solution.py:234
  (1 shorter events, 0.0 us)
Async XLA Ops:
  5.5 11.2 %all-to-all-start.1 = ((f32[4,2,8,512]{3,2,1,0:T(8,128)}), f32[4,2,8,512]{3,2,1,0:T(8,128)S(1)}, u32[]{:S(2)}, u32[]{:S(2)}) async-start(f32[4,2,8,512]{3,2,1,0:T(8,128)} %get-tuple-element.10), calls=%async_computation.1 | async-start | bytes 262144 | tf_op jit(solution)/shard_map/all_to_all | solution.py:243
  12.5 27.2 %copy-start.3 = (s32[32]{0:T(128)S(1)}, s32[32]{0:T(128)}, u32[]{:S(2)}) copy-start(s32[32]{0:T(128)} %owners_ref.3) | copy-start | bytes 388
  36.2 12.8 %all-to-all-start.2 = ((f32[4,4,2,8,512]{4,3,2,1,0:T(8,128)}), f32[4,4,2,8,512]{4,3,2,1,0:T(8,128)S(1)}, u32[]{:S(2)}, u32[]{:S(2)}) async-start(f32[4,4,2,8,512]{4,3,2,1,0:T(8,128)} %broadcast_in_dim.13), calls=%async_computation.2 | async-start | bytes 1048576 | tf_op jit(solution)/shard_map/all_to_all | solution.py:243
  55.9 30.6 %all-to-all-start.5 = ((f32[32,2,8,128]{3,2,1,0:T(8,128)}), f32[32,2,8,128]{3,2,1,0:T(8,128)S(1)}, u32[]{:S(2)}, u32[]{:S(2)}) async-start(f32[32,2,8,128]{3,2,1,0:T(8,128)} %broadcast_in_dim.28), calls=%async_computation.5 | async-start | bytes 524288 | tf_op jit(solution)/shard_map/all_to_all | solution.py:243
  86.5 8.5 %copy-start.2 = (f32[32,2,8,128]{3,2,1,0:T(8,128)}, f32[32,2,8,128]{3,2,1,0:T(8,128)S(1)}, u32[]{:S(2)}) copy-start(f32[32,2,8,128]{3,2,1,0:T(8,128)S(1)} %all-to-all-done.5.pieces_ref) | copy-start | bytes 786436
  86.5 22.8 %all-to-all-start = ((f32[32,8,512]{2,1,0:T(8,128)}), f32[32,8,512]{2,1,0:T(8,128)S(1)}, u32[]{:S(2)}, u32[]{:S(2)}) async-start(f32[32,8,512]{2,1,0:T(8,128)} %gather_blocks.3), calls=%async_computation | async-start | bytes 1048576 | tf_op jit(solution)/shard_map/all_to_all | solution.py:243
  92.9 19.9 %copy-start.4 = (s32[32]{0:T(128)S(1)}, s32[32]{0:T(128)}, u32[]{:S(2)}) copy-start(s32[32]{0:T(128)} %owners_ref.3) | copy-start | bytes 388
  109.3 4.2 %copy-start = (f32[32,8,512]{2,1,0:T(8,128)}, f32[32,8,512]{2,1,0:T(8,128)S(1)}, u32[]{:S(2)}) copy-start(f32[32,8,512]{2,1,0:T(8,128)S(1)} %all-to-all-done.current_ref) | copy-start | bytes 1572868
  109.3 12.5 %all-to-all-start.6 = ((f32[8,64,256]{2,1,0:T(8,128)}), f32[8,64,256]{2,1,0:T(8,128)S(1)}, u32[]{:S(2)}, u32[]{:S(2)}) async-start(f32[8,64,256]{2,1,0:T(8,128)} %cross.1), calls=%async_computation.6 | async-start | bytes 1048576 | tf_op jit(solution)/shard_map/all_to_all | solution.py:243
  121.8 0.8 copy-start.1

commit v2 on v0

v2 whole, which is shorter than its diff:
```python
import functools

import jax
import jax.numpy as jnp
from jax import lax
from jax.experimental import pallas as pl
from jax.experimental.pallas import tpu as pltpu
from jax.sharding import Mesh, PartitionSpec as P


F32 = jnp.float32
BF16 = jnp.bfloat16
NT = (((1,), (1,)), ((), ()))
NN = (((1,), (0,)), ((), ()))


def split(v):
    high = v.astype(BF16)
    return high, (v - high.astype(F32)).astype(BF16)


def turned(v):
    tiles = v.reshape(v.shape[0] // 8, 8, v.shape[1])
    row = lax.broadcasted_iota(jnp.int32, tiles.shape, 1)
    swapped = pltpu.roll(tiles, 4, 1)
    return jnp.where(row < 4, -swapped, swapped).reshape(v.shape)


def dot(a, b, dims=NT):
    return lax.dot_general(a, b, dims, preferred_element_type=F32)


def gather_columns(left, pivots):
    n = pivots.shape[1]
    major = pivots >> 7
    minor = pivots & 127
    pick = (lax.broadcasted_iota(jnp.int32, (128, n), 0) == major).astype(F32).astype(BF16)
    product = dot(left, jnp.concatenate([pick, pick], 0), NN).reshape(8, 16, 8, n)
    row = lax.broadcasted_iota(jnp.int32, (8, n), 0)
    found = jnp.zeros((8, 8, n), F32)
    for j in range(16):
        found = jnp.where((row + 8 * j == minor)[None], product[:, j], found)
    return found.sum(axis=1)


VMEM = pl.BlockSpec(memory_space=pltpu.VMEM)
SMEM = pl.BlockSpec(memory_space=pltpu.SMEM)
HBM = pl.BlockSpec(memory_space=pltpu.HBM)
SMALL = pltpu.CompilerParams(vmem_limit_bytes=24 << 20)


def held(v):
    return pltpu.with_memory_space_constraint(v, pltpu.VMEM)


def head_kernel(
    place_ref, panel_ref, rhs_hbm, pivots_ref, inverse_hbm, left_ref, pieces_ref, own_ref, rhs_ref, inverse_ref, sem
):
    fetch_rhs = pltpu.make_async_copy(rhs_hbm, rhs_ref, sem.at[32])
    fetch_inverse = pltpu.make_async_copy(inverse_hbm, inverse_ref, sem.at[33])
    fetch_rhs.start()
    column = pl.multiple_of(128 * place_ref[0], 128)
    copies = []
    for z in range(4):
        for k in range(8):
            source = panel_ref.at[:, pl.ds(8 * k + 2 * z, 2), :, pl.ds(column, 128)]
            copies.append(pltpu.make_async_copy(source, pieces_ref.at[z * 8 + k], sem.at[z * 8 + k]))
    for copy in copies:
        copy.start()
    fetch_inverse.start()
    fetch_rhs.wait()
    for part in range(2):
        for c in range(4):
            r = part * 4 + c
            high, low = split(rhs_ref[part, :, c, :].T)
            left_ref[pl.ds(128 * r, 128), 0:128] = high
            left_ref[pl.ds(128 * r, 128), 128:256] = low
    left = left_ref[...]
    first = jnp.concatenate([gather_columns(left, pivots_ref[0, :, 256 * k : 256 * k + 256]) for k in range(2)], 1)
    second = jnp.concatenate([gather_columns(left, pivots_ref[1, :, 256 * k : 256 * k + 256]) for k in range(2)], 1)
    own_ref[1] = second
    high, low = split(jnp.concatenate([first, turned(first)], 1))
    fetch_inverse.wait()
    w_high, w_low = split(jnp.concatenate([inverse_ref[0], inverse_ref[1]], 1))
    both = dot(jnp.concatenate([high, low], 0), w_high)
    own_ref[0] = both[0:8] + both[8:16] + dot(high, w_low)
    for copy in copies:
        copy.wait()


def in_hbm(v):
    return pltpu.with_memory_space_constraint(v, pltpu.HBM)


def head(place, panel, rhs, pivots, inverse):
    return pl.pallas_call(
        head_kernel,
        in_specs=[SMEM, HBM, HBM, VMEM, HBM],
        out_specs=[VMEM, VMEM, VMEM],
        out_shape=[
            pltpu.VMEM((1024, 256), BF16),
            jax.ShapeDtypeStruct((32, 2, 2, 8, 128), F32),
            pltpu.VMEM((2, 8, 512), F32),
        ],
        scratch_shapes=[
            pltpu.VMEM((2, 128, 4, 128), F32),
            pltpu.VMEM((2, 512, 512), F32),
            pltpu.SemaphoreType.DMA((34,)),
        ],
        name="head",
        compiler_params=SMALL,
    )(place, in_hbm(panel), in_hbm(rhs), pivots, in_hbm(inverse))


def gather_kernel(start, count, owners_ref, left_ref, pivots_ref, *rest):
    out_ref, stage_ref, sem = rest[-3:]

    def send(i):
        return pltpu.make_async_copy(stage_ref.at[i], out_ref.at[owners_ref[start + i]], sem.at[i])

    def step(i, carry):
        left = left_ref[...]
        for k in range(2):
            at = slice(256 * k, 256 * k + 256)
            stage_ref[i, :, at] = gather_columns(left, pivots_ref[start + i, :, at])
        send(i).start()
        return carry

    lax.fori_loop(0, count, step, 0, unroll=3)
    for i in range(count):
        send(i).wait()


def gather(owners, left, pivots, start, count, into=None):
    operands = [owners, held(left), pivots]
    specs = [SMEM, VMEM, VMEM]
    aliases = {}
    if into is not None:
        operands.append(into)
        specs.append(HBM)
        aliases = {3: 0}
    return pl.pallas_call(
        functools.partial(gather_kernel, start, count),
        in_specs=specs,
        out_specs=HBM,
        out_shape=pltpu.HBM((32, 8, 512), F32),
        scratch_shapes=[pltpu.VMEM((count, 8, 512), F32), pltpu.SemaphoreType.DMA((count,))],
        input_output_aliases=aliases,
        name="gather_blocks",
        compiler_params=SMALL,
    )(*operands)


def pick_kernel(owners_ref, all_ref, out_ref):
    out_ref[...] = all_ref[owners_ref[1]]


def pick(owners, everything):
    return pl.pallas_call(
        pick_kernel,
        in_specs=[SMEM, VMEM],
        out_specs=VMEM,
        out_shape=pltpu.VMEM((2, 2, 8, 128), F32),
        name="pick",
        compiler_params=SMALL,
    )(owners, held(everything))


def triple(high, low, ref):
    n = high.shape[0]
    w_high, w_low = split(jnp.concatenate([ref[0], ref[1]], 1))
    both = dot(jnp.concatenate([high, low], 0), w_high)
    return both[:n] + (both[n:] + dot(high, w_low))


def operands_kernel(me_ref, mine_ref, other_ref, high_ref, low_ref, solved_ref, second_ref):
    me = me_ref[0]
    even = (me & 1) == 0
    for j in range(16):
        at = pl.ds(16 * j, 16)
        k = (me >> 1) ^ j
        mine, other = mine_ref[k & 3, k >> 2], other_ref[k & 3, k >> 2]
        first, last = jnp.where(even, mine, other), jnp.where(even, other, mine)
        v = jnp.concatenate([first[0], last[0]], 0)
        high, low = split(jnp.concatenate([v, turned(v)], 1))
        high_ref[at, :] = high
        low_ref[at, :] = low
        solved_ref[at, :] = v
        second_ref[at, :] = jnp.concatenate([first[1], last[1]], 0)


def make_operands(me, mine, other):
    return pl.pallas_call(
        operands_kernel,
        in_specs=[SMEM, VMEM, VMEM],
        out_specs=[VMEM] * 4,
        out_shape=[pltpu.VMEM((256, 1024), BF16)] * 2 + [pltpu.VMEM((256, 512), F32)] * 2,
        name="operands",
        compiler_params=SMALL,
    )(me, held(mine), held(other))


def update_kernel(me_ref, owners_ref, high_ref, low_ref, solved_ref, panel_hbm, out_ref, panel_ref, sem):
    fetch = pltpu.make_async_copy(panel_hbm, panel_ref, sem)
    fetch.start()
    fetch.wait()
    update = triple(high_ref[...], low_ref[...], panel_ref)
    out_ref[...] = jnp.where(owners_ref[0] == me_ref[0], -solved_ref[...], update)


def make_update(me, owners, high, low, solved, panel):
    return pl.pallas_call(
        update_kernel,
        in_specs=[SMEM, SMEM, VMEM, VMEM, VMEM, HBM],
        out_specs=VMEM,
        out_shape=pltpu.VMEM((256, 512), F32),
        scratch_shapes=[pltpu.VMEM((2, 512, 512), F32), pltpu.SemaphoreType.DMA],
        name="update",
        compiler_params=SMALL,
    )(me, owners, held(high), held(low), held(solved), in_hbm(panel))


def cross_kernel(me_ref, place_ref, pieces_ref, high_ref, low_ref, out_ref, panel_ref):
    for z in range(4):
        for y in range(4):
            for part in range(2):
                for o in range(2):
                    at = pl.ds(512 * part + 128 * y, 128)
                    piece = pieces_ref[place_ref[0] ^ y, (me_ref[0] >> 3) ^ z, part, o]
                    panel_ref[pl.ds(16 * z + 8 * o, 8), at] = piece
    q_high, q_low = split(panel_ref[...])
    both = dot(jnp.concatenate([q_high, q_low], 0), high_ref[...])
    out_ref[...] = both[0:64] + both[64:128] + dot(q_high, low_ref[...])


def cross(me, place, pieces, high, low):
    return pl.pallas_call(
        cross_kernel,
        in_specs=[SMEM, SMEM] + [VMEM] * 3,
        out_specs=VMEM,
        out_shape=pltpu.VMEM((64, 256), F32),
        scratch_shapes=[pltpu.VMEM((64, 1024), F32)],
        name="cross",
        compiler_params=SMALL,
    )(me, place, held(pieces), held(high), held(low))


def tail_kernel(
    me_ref, owners_ref, base_ref, second_ref, mine_ref, other_ref, inverse_ref, panel_hbm, out_ref,
    cross_ref, panel_ref, sem,
):
    fetch = pltpu.make_async_copy(panel_hbm, panel_ref, sem)
    fetch.start()
    me = me_ref[0]
    core = me & 1
    for x in range(4):
        k = ((me >> 1) & 3) ^ x
        cross_ref[pl.ds(pl.multiple_of(128 * x + 64 * core, 64), 64), :] = mine_ref[k]
        cross_ref[pl.ds(pl.multiple_of(128 * x + 64 - 64 * core, 64), 64), :] = other_ref[k]

    def product(value, ref):
        return triple(*split(jnp.concatenate([value, turned(value)], 1)), ref)

    solved = product(second_ref[...] - cross_ref[...].T, inverse_ref)
    fetch.wait()
    update = base_ref[...] + jnp.where(owners_ref[0] == me, 0.0, product(solved, panel_ref))
    out_ref[...] = jnp.where(owners_ref[1] == me, -solved, update)


def tail(me, owners, base, second, mine, other, inverse, panel):
    return pl.pallas_call(
        tail_kernel,
        in_specs=[SMEM, SMEM] + [VMEM] * 5 + [HBM],
        out_specs=VMEM,
        out_shape=pltpu.VMEM((256, 512), F32),
        scratch_shapes=[
            pltpu.VMEM((512, 256), F32),
            pltpu.VMEM((2, 512, 512), F32),
            pltpu.SemaphoreType.DMA,
        ],
        name="tail",
        compiler_params=SMALL,
    )(me, owners, held(base), held(second), held(mine), held(other), held(inverse), in_hbm(panel))


def half_kernel(me_ref, current_ref, out_ref):
    core = me_ref[0] & 1
    for j in range(16):
        out_ref[j] = current_ref[j, 1 - core]


def half(me, current):
    return pl.pallas_call(
        half_kernel,
        in_specs=[SMEM, VMEM],
        out_specs=VMEM,
        out_shape=pltpu.VMEM((16, 8, 512), F32),
        name="half",
        compiler_params=SMALL,
    )(me, held(current))


def combine_kernel(me_ref, owners_ref, current_ref, got_ref, update_ref, out_ref):
    me = me_ref[0]
    core = me & 1
    later = (owners_ref[0] != me) & (owners_ref[1] != me)
    for j in range(16):
        own, got = current_ref[j, core], got_ref[j]
        for m in range(2):
            d = 2 * j + m
            value = jnp.where(later, jnp.where(core == m, own, got), 0.0) - update_ref[8 * d : 8 * d + 8, :]
            out_ref[0, 4 * d : 4 * d + 4, :] = value[0:4]
            out_ref[1, 4 * d : 4 * d + 4, :] = value[4:8]


def combine(me, owners, current, got, update):
    return pl.pallas_call(
        combine_kernel,
        in_specs=[SMEM, SMEM] + [VMEM] * 3,
        out_specs=VMEM,
        out_shape=jax.ShapeDtypeStruct((2, 128, 512), F32),
        name="combine",
        compiler_params=SMALL,
    )(me, owners, held(current), held(got), held(update))


def exchange(v, axis):
    return lax.all_to_all(v, axis, 0, 0, tiled=True)


def collect(v, axis):
    parts = [v]
    for k in range(1, 4):
        parts.append(lax.ppermute(v, axis, [(i, i ^ k) for i in range(4)]))
    return jnp.stack(parts)


def swap(v):
    return lax.ppermute(v, "c", [(0, 1), (1, 0)])


def shards(rhs_in, pivots, owners, panel_first, panel_second, inverse_first, inverse_second):
    row = ("z", "x", "c")
    me = lax.axis_index(row).astype(jnp.int32).reshape(1)
    place = lax.axis_index("y").astype(jnp.int32).reshape(1)
    rhs = rhs_in.reshape(2, 4, 128, 128).transpose(0, 2, 1, 3)
    piv = pivots.reshape(32, 1, 512)

    left, pieces, mine = head(place, panel_first.reshape(2, 64, 8, 512), rhs, piv, inverse_first)
    gathered = collect(mine, "z")
    pieces = exchange(pieces, row)
    gathered = collect(gathered, "x")
    blocks = gather(owners, left, piv, 2, 18)
    pieces = pick(owners, pieces)
    pieces = collect(pieces, "z")
    blocks = gather(owners, left, piv, 20, 12, blocks)
    other = swap(gathered)
    pieces = collect(pieces, "y")
    current = exchange(blocks.reshape(16, 2, 8, 512), row[:2])
    high, low, solved, second = make_operands(me, gathered, other)
    crossed = cross(me, place, pieces, high, low)
    crossed = collect(crossed, "x")
    base = make_update(me, owners, high, low, solved, panel_first)
    send = half(me, current)
    got = swap(send)
    crossed_other = swap(crossed)
    update = tail(me, owners, base, second, crossed, crossed_other, inverse_second, panel_second)
    return combine(me, owners, current, got, update)


def solution(mesh):
    fine = Mesh(mesh.devices.reshape(4, 4, 2, 4, 2), ("z", "x", "c", "y", "h"))
    row = ("z", "x", "c")
    return jax.shard_map(
        shards,
        mesh=fine,
        in_specs=(
            P(None, ("y", "h") + row, None),
            P(),
            P(),
            P(None, row, None),
            P(None, row, None),
            P(),
            P(),
        ),
        out_specs=P(None, ("y", "h"), row),
        check_vma=False,
    )
```

time: 985 us -> 101 us (0.10)
  waiting for transfers between devices: 566 us -> 29.8 us
  local copies, waits for them, and re-layouts: 303 us -> 1.64 us
  other arithmetic: 64.8 us -> 0.11 us
  starting transfers between devices: 10.5 us -> 41.2 us
  Pallas kernels: 0 us -> 27.3 us
  matrix products: 22.7 us -> 0 us
  between operations: 17.3 us -> 0.2 us
    psum x2 -> x0, waiting for transfers between devices: 551 us -> none  [broadcast(): return lax.psum(jnp.where(mine, shard, jnp.zeros_like(shard)), axis)]
    gather x2 -> x0, local copies, waits for them, and re-layouts: 209 us -> none  [shards(): ordered = jnp.take(rhs_in, jnp.take(pivots, row_index), axis=2)]
    unnamed x25 -> x12, local copies, waits for them, and re-layouts: 70.7 us -> 1.64 us
    unnamed x2 -> x0, other arithmetic: 59.1 us -> none
    ppermute x0 -> x18, waiting for transfers between devices: none -> 29.8 us  [the longest x15 29.8 us: collect(): parts.append(lax.ppermute(v, axis, [(i, i ^ k) for i in range(4)]))]
    pallas_call x0 -> x10, Pallas kernels: none -> 27.3 us  [the longest x2 13 us: gather(): pl.pallas_call(functools.partial(gather_kernel, start, count), in_specs=s...]
    ppermute x0 -> x18, starting transfers between devices: none -> 25.8 us  [the longest x15 19.5 us: collect(): parts.append(lax.ppermute(v, axis, [(i, i ^ k) for i in range(4)]))]
    dot_general x16 -> x0, matrix products: 22.7 us -> none  [multiply(): lax.dot_general(first, second, contract, precision=lax.Precision.HIGHEST,...]
  transfers between devices with their start and end apart: 3 -> 20, of which waited for: 3 -> 8; matrix products, arithmetic and copies ran while one was open for 0% -> 0% of each run, Pallas kernels for 0% -> 22%
where the time goes in v2:
time: 101 us; the launch traced here: 100 us
  starting transfers between devices  41.2 us (41%)
  waiting for transfers between devices  29.8 us (30%)
  Pallas kernels  27.3 us (27%)
  local copies, waits for them, and re-layouts  1.64 us (2%)
    ppermute x15, waiting for transfers between devices, collect(): parts.append(lax.ppermute(v, axis, [(i, i ^ k) for i in range(4)]))  29.8 us
    ppermute x15, starting transfers between devices, collect(): parts.append(lax.ppermute(v, axis, [(i, i ^ k) for i in range(4)]))  19.5 us
    all_to_all x2, starting transfers between devices, exchange(): return lax.all_to_all(v, axis, 0, 0, tiled=True)  15.3 us
    pallas_call x2, Pallas kernels, gather(): pl.pallas_call(functools.partial(gather_kernel, start, count), in_specs=s...  13 us
    ppermute x3, starting transfers between devices, swap(): return lax.ppermute(v, 'c', [(0, 1), (1, 0)])  6.37 us
    pallas_call x1, Pallas kernels, tail(): pl.pallas_call(tail_kernel, in_specs=[SMEM, SMEM] + [VMEM] * 5 + [HBM], o...  4.17 us
    pallas_call x1, Pallas kernels, head(): pl.pallas_call(head_kernel, in_specs=[SMEM, HBM, HBM, VMEM, HBM], out_spe...  4.01 us
    pallas_call x1, Pallas kernels, make_update(): pl.pallas_call(update_kernel, in_specs=[SMEM, SMEM, VMEM, VMEM, VMEM, HBM...  3.41 us
  transfers between devices with their start and end apart: 20, of which 8 were waited for; matrix products, arithmetic and copies ran while one was open for 0% of the time, Pallas kernels for 22%

profile of v2, /device:TPU:1, one launch (start us, length us, event | category | flops | bytes accessed | tf_op | source)
XLA Modules:
  0.0 100.2 jit_solution(5543208011547361242)
XLA Ops:
  0.0 0.8 copy-done.1
  0.8 4.0 %head.1 = (bf16[1024,256]{1,0:T(8,128)(2,1)S(1)}, f32[32,2,2,8,128]{4,3,2,1,0:T(8,128)}, f32[2,8,512]{2,1,0:T(8,128)S(1)}) custom-call(s32[1]{0:T(128)} %bitcast.1.place_ref, f32[2,64,8,512]{3,2,1,0:T(8,128)} %bitcast.36, f32[2,128,4,128]{3,2,1,0:T(4,128)} %bitcast.38, s32[32,1,512]{2,1,0:T(1,128)S(1)} %bitcast.30, f32[2,512,512]{2,1,0:T(8,128)} %inverse_hbm.1), custom_call_target="tpu_custom_call" | custom-call | tf_op jit(solution)/shard_map/head/pallas_call | solution.py:96
  4.9 10.0 %all-to-all-start.1 = ((f32[32,2,2,8,128]{4,3,2,1,0:T(8,128)}), f32[32,2,2,8,128]{4,3,2,1,0:T(8,128)S(1)}, u32[]{:S(2)}, u32[]{:S(2)}) async-start(f32[32,2,2,8,128]{4,3,2,1,0:T(8,128)} %get-tuple-element.18), calls=%async_computation.1 | async-start | bytes 1048576 | tf_op jit(solution)/shard_map/all_to_all | solution.py:328
  14.9 3.3 %collective-permute-start.3 = (f32[2,8,512]{2,1,0:T(8,128)S(1)}, f32[2,8,512]{2,1,0:T(8,128)S(1)}, u32[]{:S(2)}, u32[]{:S(2)}) collective-permute-start(f32[2,8,512]{2,1,0:T(8,128)S(1)} %get-tuple-element.13), channel_id=1, source_target_pairs={{0,192},{64,128},{128,64},{192,0},{1,193},{65,129},{129,65},{193,1... | collective-permute-start | bytes 98312 | tf_op jit(solution)/shard_map/ppermute | solution.py:334
  18.2 0.4 collective-permute-start.2
  18.6 9.4 %collective-permute-done.3 = f32[2,8,512]{2,1,0:T(8,128)S(1)} collective-permute-done((f32[2,8,512]{2,1,0:T(8,128)S(1)}, f32[2,8,512]{2,1,0:T(8,128)S(1)}, u32[]{:S(2)}, u32[]{:S(2)}) %collective-permute-start.3) | collective-permute-done | bytes 32800 | tf_op jit(solution)/shard_map/ppermute | solution.py:334
  28.0 0.0 collective-permute-done.1
  28.0 3.7 %collective-permute-done.2 = f32[2,8,512]{2,1,0:T(8,128)S(1)} collective-permute-done((f32[2,8,512]{2,1,0:T(8,128)S(1)}, f32[2,8,512]{2,1,0:T(8,128)S(1)}, u32[]{:S(2)}, u32[]{:S(2)}) %collective-permute-start.2) | collective-permute-done | bytes 32800 | tf_op jit(solution)/shard_map/ppermute | solution.py:334
  31.7 1.2 %collective-permute-start.4 = (f32[4,2,8,512]{3,2,1,0:T(8,128)S(1)}, f32[4,2,8,512]{3,2,1,0:T(8,128)S(1)}, u32[]{:S(2)}, u32[]{:S(2)}) collective-permute-start(f32[4,2,8,512]{3,2,1,0:T(8,128)S(1)} %get-tuple-element.20), channel_id=1, source_target_pairs={{0,16},{16,0},{32,48},{48,32},{1,17},{17,1},{33,49},{49,33},{2,18}... | collective-permute-start | bytes 393224 | tf_op jit(solution)/shard_map/ppermute | solution.py:334
  33.0 2.4 %collective-permute-start.5 = (f32[4,2,8,512]{3,2,1,0:T(8,128)S(1)}, f32[4,2,8,512]{3,2,1,0:T(8,128)S(1)}, u32[]{:S(2)}, u32[]{:S(2)}) collective-permute-start(f32[4,2,8,512]{3,2,1,0:T(8,128)S(1)} %get-tuple-element.20), channel_id=1, source_target_pairs={{0,32},{16,48},{32,0},{48,16},{1,33},{17,49},{33,1},{49,17},{2,34}... | collective-permute-start | bytes 393224 | tf_op jit(solution)/shard_map/ppermute | solution.py:334
  35.4 0.3 collective-permute-start.6
  35.7 7.6 %gather_blocks.2.rest_0_ = f32[32,8,512]{2,1,0:T(8,128)} custom-call(s32[32]{0:T(128)S(1)} %copy-done.5, bf16[1024,256]{1,0:T(8,128)(2,1)S(1)} %get-tuple-element.12.left_ref, s32[32,1,512]{2,1,0:T(1,128)S(1)} %bitcast.31), custom_call_target="tpu_custom_call" | custom-call | tf_op jit(solution)/shard_map/gather_blocks/pallas_call | solution.py:142
  43.3 5.4 %gather_blocks.3 = f32[32,8,512]{2,1,0:T(8,128)} custom-call(s32[32]{0:T(128)S(1)} %copy-done.5, bf16[1024,256]{1,0:T(8,128)(2,1)S(1)} %get-tuple-element.12.left_ref, s32[32,1,512]{2,1,0:T(1,128)S(1)} %bitcast.32, f32[32,8,512]{2,1,0:T(8,128)} %gather_blocks.2.rest_0_), custom_call_target="tpu_custom_call", output_to_operand_aliasing={{}: (3, {})} | custom-call | tf_op jit(solution)/shard_map/gather_blocks/pallas_call | solution.py:142
  48.7 0.0 all-to-all-done.1.all_ref
  48.7 5.3 %all-to-all-start = ((f32[16,2,8,512]{3,2,1,0:T(8,128)}), f32[16,2,8,512]{3,2,1,0:T(8,128)S(1)}, u32[]{:S(2)}, u32[]{:S(2)}) async-start(f32[16,2,8,512]{3,2,1,0:T(8,128)} %bitcast.37), calls=%async_computation | async-start | bytes 1048576 | tf_op jit(solution)/shard_map/all_to_all | solution.py:328
  54.1 0.0 collective-permute-done.4
  54.1 0.0 collective-permute-done.5
  54.1 1.8 %collective-permute-start.7 = (f32[4,4,2,8,512]{4,3,2,1,0:T(8,128)S(1)}, f32[4,4,2,8,512]{4,3,2,1,0:T(8,128)S(1)}, u32[]{:S(2)}, u32[]{:S(2)}) collective-permute-start(f32[4,4,2,8,512]{4,3,2,1,0:T(8,128)S(1)} %pad_maximum_fusion.mine_ref), channel_id=1, source_target_pairs={{0,8},{8,0},{1,9},{9,1},{2,10},{10,2},{3,11},{11,3},{4,12},{12,4},... | collective-permute-start | bytes 1572872 | tf_op jit(solution)/shard_map/ppermute | solution.py:339
  55.9 0.5 pick.1
  56.5 1.7 %collective-permute-start.8 = (f32[2,2,8,128]{3,2,1,0:T(8,128)S(1)}, f32[2,2,8,128]{3,2,1,0:T(8,128)S(1)}, u32[]{:S(2)}, u32[]{:S(2)}) collective-permute-start(f32[2,2,8,128]{3,2,1,0:T(8,128)S(1)} %pick.1), channel_id=1, source_target_pairs={{0,64},{64,0},{128,192},{192,128},{1,65},{65,1},{129,193},{193,129... | collective-permute-start | bytes 49160 | tf_op jit(solution)/shard_map/ppermute | solution.py:334
  58.2 2.1 %collective-permute-start.9 = (f32[2,2,8,128]{3,2,1,0:T(8,128)S(1)}, f32[2,2,8,128]{3,2,1,0:T(8,128)S(1)}, u32[]{:S(2)}, u32[]{:S(2)}) collective-permute-start(f32[2,2,8,128]{3,2,1,0:T(8,128)S(1)} %pick.1), channel_id=1, source_target_pairs={{0,128},{64,192},{128,0},{192,64},{1,129},{65,193},{129,1},{193,65... | collective-permute-start | bytes 49160 | tf_op jit(solution)/shard_map/ppermute | solution.py:334
  60.3 0.1 collective-permute-start.10
  60.4 1.3 %collective-permute-done.8 = f32[2,2,8,128]{3,2,1,0:T(8,128)S(1)} collective-permute-done((f32[2,2,8,128]{3,2,1,0:T(8,128)S(1)}, f32[2,2,8,128]{3,2,1,0:T(8,128)S(1)}, u32[]{:S(2)}, u32[]{:S(2)}) %collective-permute-start.8) | collective-permute-done | bytes 16416 | tf_op jit(solution)/shard_map/ppermute | solution.py:334
  61.7 7.3 %collective-permute-done.9 = f32[2,2,8,128]{3,2,1,0:T(8,128)S(1)} collective-permute-done((f32[2,2,8,128]{3,2,1,0:T(8,128)S(1)}, f32[2,2,8,128]{3,2,1,0:T(8,128)S(1)}, u32[]{:S(2)}, u32[]{:S(2)}) %collective-permute-start.9) | collective-permute-done | bytes 16416 | tf_op jit(solution)/shard_map/ppermute | solution.py:334
  69.1 0.0 collective-permute-done.10
  69.1 1.4 %collective-permute-start.11 = (f32[4,2,2,8,128]{4,3,2,1,0:T(8,128)S(1)}, f32[4,2,2,8,128]{4,3,2,1,0:T(8,128)S(1)}, u32[]{:S(2)}, u32[]{:S(2)}) collective-permute-start(f32[4,2,2,8,128]{4,3,2,1,0:T(8,128)S(1)} %get-tuple-element.22), channel_id=1, source_target_pairs={{0,2},{2,0},{4,6},{6,4},{1,3},{3,1},{5,7},{7,5},{8,10},{10,8},{12,... | collective-permute-start | bytes 196616 | tf_op jit(solution)/shard_map/ppermute | solution.py:334
  70.4 2.6 %collective-permute-start.12 = (f32[4,2,2,8,128]{4,3,2,1,0:T(8,128)S(1)}, f32[4,2,2,8,128]{4,3,2,1,0:T(8,128)S(1)}, u32[]{:S(2)}, u32[]{:S(2)}) collective-permute-start(f32[4,2,2,8,128]{4,3,2,1,0:T(8,128)S(1)} %get-tuple-element.22), channel_id=1, source_target_pairs={{0,4},{2,6},{4,0},{6,2},{1,5},{3,7},{5,1},{7,3},{8,12},{10,14},{12... | collective-permute-start | bytes 196616 | tf_op jit(solution)/shard_map/ppermute | solution.py:334
  73.1 0.0 collective-permute-start.13
  73.1 0.0 collective-permute-done.7.other_ref
  73.1 0.2 operands.1
  73.3 0.0 copy-start.3
  73.3 0.8 copy-done.3
  74.1 1.3 %collective-permute-done.12 = f32[4,2,2,8,128]{4,3,2,1,0:T(8,128)S(1)} collective-permute-done((f32[4,2,2,8,128]{4,3,2,1,0:T(8,128)S(1)}, f32[4,2,2,8,128]{4,3,2,1,0:T(8,128)S(1)}, u32[]{:S(2)}, u32[]{:S(2)}) %collective-permute-start.12) | collective-permute-done | bytes 65568 | tf_op jit(solution)/shard_map/ppermute | solution.py:334
  75.4 2.7 %collective-permute-done.13 = f32[4,2,2,8,128]{4,3,2,1,0:T(8,128)S(1)} collective-permute-done((f32[4,2,2,8,128]{4,3,2,1,0:T(8,128)S(1)}, f32[4,2,2,8,128]{4,3,2,1,0:T(8,128)S(1)}, u32[]{:S(2)}, u32[]{:S(2)}) %collective-permute-start.13) | collective-permute-done | bytes 65568 | tf_op jit(solution)/shard_map/ppermute | solution.py:334
  78.1 0.5 cross.1
  78.6 1.3 %collective-permute-start.14 = (f32[64,256]{1,0:T(8,128)S(1)}, f32[64,256]{1,0:T(8,128)S(1)}, u32[]{:S(2)}, u32[]{:S(2)}) collective-permute-start(f32[64,256]{1,0:T(8,128)S(1)} %cross.1), channel_id=1, source_target_pairs={{0,16},{16,0},{32,48},{48,32},{1,17},{17,1},{33,49},{49,33},{2,18}... | collective-permute-start | bytes 196616 | tf_op jit(solution)/shard_map/ppermute | solution.py:334
  79.8 2.3 %collective-permute-start.15 = (f32[64,256]{1,0:T(8,128)S(1)}, f32[64,256]{1,0:T(8,128)S(1)}, u32[]{:S(2)}, u32[]{:S(2)}) collective-permute-start(f32[64,256]{1,0:T(8,128)S(1)} %cross.1), channel_id=1, source_target_pairs={{0,32},{16,48},{32,0},{48,16},{1,33},{17,49},{33,1},{49,17},{2,34}... | collective-permute-start | bytes 196616 | tf_op jit(solution)/shard_map/ppermute | solution.py:334
  82.2 0.4 collective-permute-start.16
  82.5 0.0 collective-permute-done.14
  82.5 2.0 %collective-permute-done.15 = f32[64,256]{1,0:T(8,128)S(1)} collective-permute-done((f32[64,256]{1,0:T(8,128)S(1)}, f32[64,256]{1,0:T(8,128)S(1)}, u32[]{:S(2)}, u32[]{:S(2)}) %collective-permute-start.15) | collective-permute-done | bytes 65568 | tf_op jit(solution)/shard_map/ppermute | solution.py:334
  84.5 2.0 %collective-permute-done.16 = f32[64,256]{1,0:T(8,128)S(1)} collective-permute-done((f32[64,256]{1,0:T(8,128)S(1)}, f32[64,256]{1,0:T(8,128)S(1)}, u32[]{:S(2)}, u32[]{:S(2)}) %collective-permute-start.16) | collective-permute-done | bytes 65568 | tf_op jit(solution)/shard_map/ppermute | solution.py:334
  86.5 4.5 %collective-permute-start.17 = (f32[4,64,256]{2,1,0:T(8,128)S(1)}, f32[4,64,256]{2,1,0:T(8,128)S(1)}, u32[]{:S(2)}, u32[]{:S(2)}) collective-permute-start(f32[4,64,256]{2,1,0:T(8,128)S(1)} %pad_maximum_fusion.2.mine_ref), channel_id=1, source_target_pairs={{0,8},{8,0},{1,9},{9,1},{2,10},{10,2},{3,11},{11,3},{4,12},{12,4},... | collective-permute-start | bytes 786440 | tf_op jit(solution)/shard_map/ppermute | solution.py:339
  91.0 0.0 all-to-all-done.current_ref
  91.0 0.1 collective-permute-start
  91.1 3.4 %update.1.base_ref = f32[256,512]{1,0:T(8,128)S(1)} custom-call(s32[1]{0:T(128)} %bitcast.me_ref, s32[32]{0:T(128)S(1)} %copy-done.5, bf16[256,1024]{1,0:T(8,128)(2,1)S(1)} %get-tuple-element.14.high_ref, bf16[256,1024]{1,0:T(8,128)(2,1)S(1)} %get-tuple-element.15.low_ref, f32[256,512]{1,0:T(8,128)S(1)} %get-tuple-element.16.solved_ref, f32[2,512,512]{2,1,0:T(8,128)} %panel_hbm.2), custom_call_target="tpu_custom_call" | custom-call | tf_op jit(solution)/shard_map/update/pallas_call | solution.py:212
  94.6 0.0 collective-permute-done.17.other_ref
  94.6 4.2 %tail.1.update_ref = f32[256,512]{1,0:T(8,128)S(1)} custom-call(s32[1]{0:T(128)} %bitcast.me_ref, s32[32]{0:T(128)S(1)} %copy-done.5, f32[256,512]{1,0:T(8,128)S(1)} %update.1.base_ref, f32[256,512]{1,0:T(8,128)S(1)} %copy-done.4, f32[4,64,256]{2,1,0:T(8,128)S(1)} %pad_maximum_fusion.2.mine_ref, f32[4,64,256]{2,1,0:T(8,128)S(1)} %collective-permute-done.17.other_ref, ...), custom_call_target="tpu_custom_call" | custom-call | tf_op jit(solution)/shard_map/tail/pallas_call | solution.py:271
  98.8 1.4 %combine.1 = f32[2,128,512]{2,1,0:T(8,128)} custom-call(s32[1]{0:T(128)} %bitcast.me_ref, s32[32]{0:T(128)S(1)} %copy-done.5, f32[16,2,8,512]{3,2,1,0:T(8,128)S(1)} %all-to-all-done.current_ref, f32[16,8,512]{2,1,0:T(8,128)S(1)} %collective-permute-done.got_ref, f32[256,512]{1,0:T(8,128)S(1)} %tail.1.update_ref), custom_call_target="tpu_custom_call" | custom-call | tf_op jit(solution)/shard_map/combine/pallas_call | solution.py:317
  (19 shorter events, 0.1 us)
Async XLA Ops:
  0.0 0.8 copy-start.1
  0.8 34.9 %copy-start.2 = (s32[16384]{0:T(1024)S(1)}, s32[16384]{0:T(1024)}, u32[]{:S(2)}) copy-start(s32[16384]{0:T(1024)} %param.8) | copy-start | bytes 196612
  0.8 34.9 %copy-start.5 = (s32[32]{0:T(128)S(1)}, s32[32]{0:T(128)}, u32[]{:S(2)}) copy-start(s32[32]{0:T(128)} %owners_ref.11) | copy-start | bytes 388
  4.9 43.9 %all-to-all-start.1 = ((f32[32,2,2,8,128]{4,3,2,1,0:T(8,128)}), f32[32,2,2,8,128]{4,3,2,1,0:T(8,128)S(1)}, u32[]{:S(2)}, u32[]{:S(2)}) async-start(f32[32,2,2,8,128]{4,3,2,1,0:T(8,128)} %get-tuple-element.18), calls=%async_computation.1 | async-start | bytes 1048576 | tf_op jit(solution)/shard_map/all_to_all | solution.py:328
  14.9 13.1 %collective-permute-start.3 = (f32[2,8,512]{2,1,0:T(8,128)S(1)}, f32[2,8,512]{2,1,0:T(8,128)S(1)}, u32[]{:S(2)}, u32[]{:S(2)}) collective-permute-start(f32[2,8,512]{2,1,0:T(8,128)S(1)} %get-tuple-element.13), channel_id=1, source_target_pairs={{0,192},{64,128},{128,64},{192,0},{1,193},{65,129},{129,65},{193,1... | collective-permute-start | bytes 98312 | tf_op jit(solution)/shard_map/ppermute | solution.py:334
  18.2 9.8 %collective-permute-start.1 = (f32[2,8,512]{2,1,0:T(8,128)S(1)}, f32[2,8,512]{2,1,0:T(8,128)S(1)}, u32[]{:S(2)}, u32[]{:S(2)}) collective-permute-start(f32[2,8,512]{2,1,0:T(8,128)S(1)} %get-tuple-element.13), channel_id=1, source_target_pairs={{0,64},{64,0},{128,192},{192,128},{1,65},{65,1},{129,193},{193,129... | collective-permute-start | bytes 98312 | tf_op jit(solution)/shard_map/ppermute | solution.py:334
  18.2 13.5 %collective-permute-start.2 = (f32[2,8,512]{2,1,0:T(8,128)S(1)}, f32[2,8,512]{2,1,0:T(8,128)S(1)}, u32[]{:S(2)}, u32[]{:S(2)}) collective-permute-start(f32[2,8,512]{2,1,0:T(8,128)S(1)} %get-tuple-element.13), channel_id=1, source_target_pairs={{0,128},{64,192},{128,0},{192,64},{1,129},{65,193},{129,1},{193,65... | collective-permute-start | bytes 98312 | tf_op jit(solution)/shard_map/ppermute | solution.py:334
  31.7 22.3 %collective-permute-start.4 = (f32[4,2,8,512]{3,2,1,0:T(8,128)S(1)}, f32[4,2,8,512]{3,2,1,0:T(8,128)S(1)}, u32[]{:S(2)}, u32[]{:S(2)}) collective-permute-start(f32[4,2,8,512]{3,2,1,0:T(8,128)S(1)} %get-tuple-element.20), channel_id=1, source_target_pairs={{0,16},{16,0},{32,48},{48,32},{1,17},{17,1},{33,49},{49,33},{2,18}... | collective-permute-start | bytes 393224 | tf_op jit(solution)/shard_map/ppermute | solution.py:334
  33.0 21.1 %collective-permute-start.5 = (f32[4,2,8,512]{3,2,1,0:T(8,128)S(1)}, f32[4,2,8,512]{3,2,1,0:T(8,128)S(1)}, u32[]{:S(2)}, u32[]{:S(2)}) collective-permute-start(f32[4,2,8,512]{3,2,1,0:T(8,128)S(1)} %get-tuple-element.20), channel_id=1, source_target_pairs={{0,32},{16,48},{32,0},{48,16},{1,33},{17,49},{33,1},{49,17},{2,34}... | collective-permute-start | bytes 393224 | tf_op jit(solution)/shard_map/ppermute | solution.py:334
  35.4 18.7 %collective-permute-start.6 = (f32[4,2,8,512]{3,2,1,0:T(8,128)S(1)}, f32[4,2,8,512]{3,2,1,0:T(8,128)S(1)}, u32[]{:S(2)}, u32[]{:S(2)}) collective-permute-start(f32[4,2,8,512]{3,2,1,0:T(8,128)S(1)} %get-tuple-element.20), channel_id=1, source_target_pairs={{0,48},{16,32},{32,16},{48,0},{1,49},{17,33},{33,17},{49,1},{2,50}... | collective-permute-start | bytes 393224 | tf_op jit(solution)/shard_map/ppermute | solution.py:334
  48.7 42.3 %all-to-all-start = ((f32[16,2,8,512]{3,2,1,0:T(8,128)}), f32[16,2,8,512]{3,2,1,0:T(8,128)S(1)}, u32[]{:S(2)}, u32[]{:S(2)}) async-start(f32[16,2,8,512]{3,2,1,0:T(8,128)} %bitcast.37), calls=%async_computation | async-start | bytes 1048576 | tf_op jit(solution)/shard_map/all_to_all | solution.py:328
  54.1 18.9 %collective-permute-start.7 = (f32[4,4,2,8,512]{4,3,2,1,0:T(8,128)S(1)}, f32[4,4,2,8,512]{4,3,2,1,0:T(8,128)S(1)}, u32[]{:S(2)}, u32[]{:S(2)}) collective-permute-start(f32[4,4,2,8,512]{4,3,2,1,0:T(8,128)S(1)} %pad_maximum_fusion.mine_ref), channel_id=1, source_target_pairs={{0,8},{8,0},{1,9},{9,1},{2,10},{10,2},{3,11},{11,3},{4,12},{12,4},... | collective-permute-start | bytes 1572872 | tf_op jit(solution)/shard_map/ppermute | solution.py:339
  56.5 5.2 %collective-permute-start.8 = (f32[2,2,8,128]{3,2,1,0:T(8,128)S(1)}, f32[2,2,8,128]{3,2,1,0:T(8,128)S(1)}, u32[]{:S(2)}, u32[]{:S(2)}) collective-permute-start(f32[2,2,8,128]{3,2,1,0:T(8,128)S(1)} %pick.1), channel_id=1, source_target_pairs={{0,64},{64,0},{128,192},{192,128},{1,65},{65,1},{129,193},{193,129... | collective-permute-start | bytes 49160 | tf_op jit(solution)/shard_map/ppermute | solution.py:334
  58.2 10.9 %collective-permute-start.9 = (f32[2,2,8,128]{3,2,1,0:T(8,128)S(1)}, f32[2,2,8,128]{3,2,1,0:T(8,128)S(1)}, u32[]{:S(2)}, u32[]{:S(2)}) collective-permute-start(f32[2,2,8,128]{3,2,1,0:T(8,128)S(1)} %pick.1), channel_id=1, source_target_pairs={{0,128},{64,192},{128,0},{192,64},{1,129},{65,193},{129,1},{193,65... | collective-permute-start | bytes 49160 | tf_op jit(solution)/shard_map/ppermute | solution.py:334
  60.3 8.8 %collective-permute-start.10 = (f32[2,2,8,128]{3,2,1,0:T(8,128)S(1)}, f32[2,2,8,128]{3,2,1,0:T(8,128)S(1)}, u32[]{:S(2)}, u32[]{:S(2)}) collective-permute-start(f32[2,2,8,128]{3,2,1,0:T(8,128)S(1)} %pick.1), channel_id=1, source_target_pairs={{0,192},{64,128},{128,64},{192,0},{1,193},{65,129},{129,65},{193,1... | collective-permute-start | bytes 49160 | tf_op jit(solution)/shard_map/ppermute | solution.py:334
  69.1 5.0 %collective-permute-start.11 = (f32[4,2,2,8,128]{4,3,2,1,0:T(8,128)S(1)}, f32[4,2,2,8,128]{4,3,2,1,0:T(8,128)S(1)}, u32[]{:S(2)}, u32[]{:S(2)}) collective-permute-start(f32[4,2,2,8,128]{4,3,2,1,0:T(8,128)S(1)} %get-tuple-element.22), channel_id=1, source_target_pairs={{0,2},{2,0},{4,6},{6,4},{1,3},{3,1},{5,7},{7,5},{8,10},{10,8},{12,... | collective-permute-start | bytes 196616 | tf_op jit(solution)/shard_map/ppermute | solution.py:334
  70.4 5.0 %collective-permute-start.12 = (f32[4,2,2,8,128]{4,3,2,1,0:T(8,128)S(1)}, f32[4,2,2,8,128]{4,3,2,1,0:T(8,128)S(1)}, u32[]{:S(2)}, u32[]{:S(2)}) collective-permute-start(f32[4,2,2,8,128]{4,3,2,1,0:T(8,128)S(1)} %get-tuple-element.22), channel_id=1, source_target_pairs={{0,4},{2,6},{4,0},{6,2},{1,5},{3,7},{5,1},{7,3},{8,12},{10,14},{12... | collective-permute-start | bytes 196616 | tf_op jit(solution)/shard_map/ppermute | solution.py:334
  73.1 5.0 %collective-permute-start.13 = (f32[4,2,2,8,128]{4,3,2,1,0:T(8,128)S(1)}, f32[4,2,2,8,128]{4,3,2,1,0:T(8,128)S(1)}, u32[]{:S(2)}, u32[]{:S(2)}) collective-permute-start(f32[4,2,2,8,128]{4,3,2,1,0:T(8,128)S(1)} %get-tuple-element.22), channel_id=1, source_target_pairs={{0,6},{2,4},{4,2},{6,0},{1,7},{3,5},{5,3},{7,1},{8,14},{10,12},{12... | collective-permute-start | bytes 196616 | tf_op jit(solution)/shard_map/ppermute | solution.py:334
  73.3 0.8 copy-start.3
  78.6 3.9 %collective-permute-start.14 = (f32[64,256]{1,0:T(8,128)S(1)}, f32[64,256]{1,0:T(8,128)S(1)}, u32[]{:S(2)}, u32[]{:S(2)}) collective-permute-start(f32[64,256]{1,0:T(8,128)S(1)} %cross.1), channel_id=1, source_target_pairs={{0,16},{16,0},{32,48},{48,32},{1,17},{17,1},{33,49},{49,33},{2,18}... | collective-permute-start | bytes 196616 | tf_op jit(solution)/shard_map/ppermute | solution.py:334
  79.8 4.7 %collective-permute-start.15 = (f32[64,256]{1,0:T(8,128)S(1)}, f32[64,256]{1,0:T(8,128)S(1)}, u32[]{:S(2)}, u32[]{:S(2)}) collective-permute-start(f32[64,256]{1,0:T(8,128)S(1)} %cross.1), channel_id=1, source_target_pairs={{0,32},{16,48},{32,0},{48,16},{1,33},{17,49},{33,1},{49,17},{2,34}... | collective-permute-start | bytes 196616 | tf_op jit(solution)/shard_map/ppermute | solution.py:334
  82.2 4.3 %collective-permute-start.16 = (f32[64,256]{1,0:T(8,128)S(1)}, f32[64,256]{1,0:T(8,128)S(1)}, u32[]{:S(2)}, u32[]{:S(2)}) collective-permute-start(f32[64,256]{1,0:T(8,128)S(1)} %cross.1), channel_id=1, source_target_pairs={{0,48},{16,32},{32,16},{48,0},{1,49},{17,33},{33,17},{49,1},{2,50}... | collective-permute-start | bytes 196616 | tf_op jit(solution)/shard_map/ppermute | solution.py:334
  86.5 8.1 %collective-permute-start.17 = (f32[4,64,256]{2,1,0:T(8,128)S(1)}, f32[4,64,256]{2,1,0:T(8,128)S(1)}, u32[]{:S(2)}, u32[]{:S(2)}) collective-permute-start(f32[4,64,256]{2,1,0:T(8,128)S(1)} %pad_maximum_fusion.2.mine_ref), channel_id=1, source_target_pairs={{0,8},{8,0},{1,9},{9,1},{2,10},{10,2},{3,11},{11,3},{4,12},{12,4},... | collective-permute-start | bytes 786440 | tf_op jit(solution)/shard_map/ppermute | solution.py:339
  91.0 7.8 %collective-permute-start = (f32[16,8,512]{2,1,0:T(8,128)S(1)}, f32[16,8,512]{2,1,0:T(8,128)S(1)}, u32[]{:S(2)}, u32[]{:S(2)}) collective-permute-start(f32[16,8,512]{2,1,0:T(8,128)S(1)} %half.1), channel_id=1, source_target_pairs={{0,8},{8,0},{1,9},{9,1},{2,10},{10,2},{3,11},{11,3},{4,12},{12,4},... | collective-permute-start | bytes 786440 | tf_op jit(solution)/shard_map/ppermute | solution.py:339
  91.1 3.4 %copy-start = (f32[2,512,512]{2,1,0:T(8,128)S(1)}, f32[2,512,512]{2,1,0:T(8,128)}, u32[]{:S(2)}) copy-start(f32[2,512,512]{2,1,0:T(8,128)} %inverse_ref.1) | copy-start | bytes 6291460
  91.1 3.4 %copy-start.4 = (f32[256,512]{1,0:T(8,128)S(1)}, f32[256,512]{1,0:T(8,128)}, u32[]{:S(2)}) copy-start(f32[256,512]{1,0:T(8,128)} %copy-done.3) | copy-start | bytes 1572868

commit v3 on v2

v3 whole, which is shorter than its diff:
```python
import functools

import jax
import jax.numpy as jnp
from jax import lax
from jax.experimental import pallas as pl
from jax.experimental.pallas import tpu as pltpu
from jax.sharding import Mesh, PartitionSpec as P


F32 = jnp.float32
BF16 = jnp.bfloat16
NT = (((1,), (1,)), ((), ()))
NN = (((1,), (0,)), ((), ()))


def split(v):
    high = v.astype(BF16)
    return high, (v - high.astype(F32)).astype(BF16)


def turned(v):
    tiles = v.reshape(v.shape[0] // 8, 8, v.shape[1])
    row = lax.broadcasted_iota(jnp.int32, tiles.shape, 1)
    swapped = pltpu.roll(tiles, 4, 1)
    return jnp.where(row < 4, -swapped, swapped).reshape(v.shape)


def dot(a, b, dims=NT):
    return lax.dot_general(a, b, dims, preferred_element_type=F32)


def gather_columns(left, pivots):
    n = pivots.shape[1]
    major = pivots >> 7
    minor = pivots & 127
    pick = (lax.broadcasted_iota(jnp.int32, (128, n), 0) == major).astype(F32).astype(BF16)
    product = dot(left, jnp.concatenate([pick, pick], 0), NN).reshape(8, 16, 8, n)
    row = lax.broadcasted_iota(jnp.int32, (8, n), 0)
    found = jnp.zeros((8, 8, n), F32)
    for j in range(16):
        found = jnp.where((row + 8 * j == minor)[None], product[:, j], found)
    return found.sum(axis=1)


VMEM = pl.BlockSpec(memory_space=pltpu.VMEM)
SMEM = pl.BlockSpec(memory_space=pltpu.SMEM)
HBM = pl.BlockSpec(memory_space=pltpu.HBM)
SMALL = pltpu.CompilerParams(vmem_limit_bytes=24 << 20)


def fetches(source, target, sem, first, count):
    rows = source.shape[1] // count
    return [
        pltpu.make_async_copy(
            source.at[:, pl.ds(rows * i, rows)], target.at[:, pl.ds(rows * i, rows)], sem.at[first + i]
        )
        for i in range(count)
    ]


def held(v):
    return pltpu.with_memory_space_constraint(v, pltpu.VMEM)


def pieces_kernel(place_ref, panel_ref, out_ref, stage_ref, sem):
    column = pl.multiple_of(128 * place_ref[0], 128)
    copies = []
    stores = []
    for k in range(8):
        source = panel_ref.at[:, pl.ds(8 * k, 8), :, pl.ds(column, 128)]
        copies.append(pltpu.make_async_copy(source, stage_ref.at[k], sem.at[k]))
        stores.append(pltpu.make_async_copy(stage_ref.at[k], out_ref.at[k], sem.at[8 + k]))
    for copy in copies:
        copy.start()
    for copy, store in zip(copies, stores):
        copy.wait()
        store.start()
    for store in stores:
        store.wait()


def make_pieces(place, panel):
    return pl.pallas_call(
        pieces_kernel,
        in_specs=[SMEM, HBM],
        out_specs=HBM,
        out_shape=pltpu.HBM((8, 2, 8, 8, 128), F32),
        scratch_shapes=[pltpu.VMEM((8, 2, 8, 8, 128), F32), pltpu.SemaphoreType.DMA((16,))],
        name="pieces",
        compiler_params=SMALL,
    )(place, in_hbm(panel))


def head_kernel(rhs_hbm, pivots_ref, inverse_ref, left_ref, own_ref, rhs_ref, sem):
    copies = fetches(rhs_hbm, rhs_ref, sem, 0, 8)
    for copy in copies:
        copy.start()
    for copy in copies:
        copy.wait()
    for part in range(2):
        for c in range(4):
            r = part * 4 + c
            high, low = split(rhs_ref[part, :, c, :].T)
            left_ref[pl.ds(128 * r, 128), 0:128] = high
            left_ref[pl.ds(128 * r, 128), 128:256] = low
    left = left_ref[...]
    first = jnp.concatenate([gather_columns(left, pivots_ref[0, :, 256 * k : 256 * k + 256]) for k in range(2)], 1)
    second = jnp.concatenate([gather_columns(left, pivots_ref[1, :, 256 * k : 256 * k + 256]) for k in range(2)], 1)
    own_ref[1] = second
    high, low = split(jnp.concatenate([first, turned(first)], 1))
    w_high, w_low = split(jnp.concatenate([inverse_ref[0], inverse_ref[1]], 1))
    both = dot(jnp.concatenate([high, low], 0), w_high)
    own_ref[0] = both[0:8] + both[8:16] + dot(high, w_low)


def in_hbm(v):
    return pltpu.with_memory_space_constraint(v, pltpu.HBM)


def head(rhs, pivots, inverse):
    return pl.pallas_call(
        head_kernel,
        in_specs=[HBM, VMEM, VMEM],
        out_specs=[VMEM] * 2,
        out_shape=[pltpu.VMEM((1024, 256), BF16), pltpu.VMEM((2, 8, 512), F32)],
        scratch_shapes=[pltpu.VMEM((2, 128, 4, 128), F32), pltpu.SemaphoreType.DMA((8,))],
        name="head",
        compiler_params=SMALL,
    )(in_hbm(rhs), held(pivots), held(inverse))


def gather_kernel(start, count, owners_ref, left_ref, pivots_ref, *rest):
    out_ref, stage_ref, sem = rest[-3:]

    def send(i):
        return pltpu.make_async_copy(stage_ref.at[i], out_ref.at[owners_ref[start + i]], sem.at[i])

    def step(i, carry):
        left = left_ref[...]
        for k in range(2):
            at = slice(256 * k, 256 * k + 256)
            stage_ref[i, :, at] = gather_columns(left, pivots_ref[start + i, :, at])
        send(i).start()
        return carry

    lax.fori_loop(0, count, step, 0, unroll=6)
    for i in range(count):
        send(i).wait()


def gather(owners, left, pivots, start, count, into=None):
    operands = [owners, held(left), pivots]
    specs = [SMEM, VMEM, VMEM]
    aliases = {}
    if into is not None:
        operands.append(into)
        specs.append(HBM)
        aliases = {3: 0}
    return pl.pallas_call(
        functools.partial(gather_kernel, start, count),
        in_specs=specs,
        out_specs=HBM,
        out_shape=pltpu.HBM((32, 8, 512), F32),
        scratch_shapes=[pltpu.VMEM((count, 8, 512), F32), pltpu.SemaphoreType.DMA((count,))],
        input_output_aliases=aliases,
        name="gather_blocks",
        compiler_params=SMALL,
    )(*operands)


def pick_kernel(owners_ref, all_ref, out_ref):
    out_ref[...] = all_ref[owners_ref[1] & 7]


def pick(owners, everything):
    return pl.pallas_call(
        pick_kernel,
        in_specs=[SMEM, VMEM],
        out_specs=VMEM,
        out_shape=pltpu.VMEM((2, 8, 8, 128), F32),
        name="pick",
        compiler_params=SMALL,
    )(owners, held(everything))


def choose_kernel(me_ref, owners_ref, own_ref, one_ref, two_ref, three_ref, out_ref):
    k = (me_ref[0] ^ owners_ref[1]) >> 3
    low = jnp.where((k & 1) == 0, own_ref[...], one_ref[...])
    high = jnp.where((k & 1) == 0, two_ref[...], three_ref[...])
    out_ref[...] = jnp.where(k < 2, low, high)


def choose(me, owners, parts):
    return pl.pallas_call(
        choose_kernel,
        in_specs=[SMEM, SMEM] + [VMEM] * 4,
        out_specs=VMEM,
        out_shape=pltpu.VMEM((2, 8, 8, 128), F32),
        name="choose",
        compiler_params=SMALL,
    )(me, owners, *[held(p) for p in parts])


def triple(high, low, ref):
    n = high.shape[0]
    w_high, w_low = split(jnp.concatenate([ref[0], ref[1]], 1))
    both = dot(jnp.concatenate([high, low], 0), w_high)
    return both[:n] + (both[n:] + dot(high, w_low))


def operands_kernel(me_ref, mine_ref, other_ref, high_ref, low_ref, solved_ref, second_hbm, second_ref, sem):
    me = me_ref[0]
    even = (me & 1) == 0

    def arranged(j, n):
        k = (me >> 1) ^ j
        k = ((k & 1) << 3) | (k & 4) | (k & 2) | (k >> 3)
        mine, other = mine_ref[k, n], other_ref[k, n]
        return jnp.concatenate([jnp.where(even, mine, other), jnp.where(even, other, mine)], 0)

    for j in range(16):
        second_ref[pl.ds(16 * j, 16), :] = arranged(j, 1)
    store = pltpu.make_async_copy(second_ref, second_hbm, sem)
    store.start()
    for j in range(16):
        at = pl.ds(16 * j, 16)
        v = arranged(j, 0)
        high, low = split(jnp.concatenate([v, turned(v)], 1))
        high_ref[at, :] = high
        low_ref[at, :] = low
        solved_ref[at, :] = v
    store.wait()


def make_operands(me, mine, other):
    return pl.pallas_call(
        operands_kernel,
        in_specs=[SMEM, VMEM, VMEM],
        out_specs=[VMEM] * 3 + [HBM],
        out_shape=[pltpu.VMEM((256, 1024), BF16)] * 2 + [pltpu.VMEM((256, 512), F32), pltpu.HBM((256, 512), F32)],
        scratch_shapes=[pltpu.VMEM((256, 512), F32), pltpu.SemaphoreType.DMA],
        name="operands",
        compiler_params=SMALL,
    )(me, held(mine.reshape(16, 2, 8, 512)), held(other.reshape(16, 2, 8, 512)))


def update_kernel(me_ref, owners_ref, high_ref, low_ref, solved_ref, panel_hbm, out_ref, panel_ref, sem):
    copies = fetches(panel_hbm, panel_ref, sem, 0, 8)
    for copy in copies:
        copy.start()
    for copy in copies:
        copy.wait()
    update = triple(high_ref[...], low_ref[...], panel_ref)
    out_ref[...] = jnp.where(owners_ref[0] == me_ref[0], -solved_ref[...], update)


def make_update(me, owners, high, low, solved, panel):
    return pl.pallas_call(
        update_kernel,
        in_specs=[SMEM, SMEM, VMEM, VMEM, VMEM, HBM],
        out_specs=VMEM,
        out_shape=pltpu.VMEM((256, 512), F32),
        scratch_shapes=[pltpu.VMEM((2, 512, 512), F32), pltpu.SemaphoreType.DMA((8,))],
        name="update",
        compiler_params=SMALL,
    )(me, owners, held(high), held(low), held(solved), in_hbm(panel))


def cross_kernel(place_ref, pieces_ref, high_ref, low_ref, out_ref, panel_ref):
    for y in range(4):
        for part in range(2):
            piece = pieces_ref[place_ref[0] ^ y, part]
            panel_ref[:, pl.ds(512 * part + 128 * y, 128)] = piece.reshape(64, 128)
    q_high, q_low = split(panel_ref[...])
    both = dot(jnp.concatenate([q_high, q_low], 0), high_ref[...])
    out_ref[...] = both[0:64] + both[64:128] + dot(q_high, low_ref[...])


def cross(place, pieces, high, low):
    return pl.pallas_call(
        cross_kernel,
        in_specs=[SMEM] + [VMEM] * 3,
        out_specs=VMEM,
        out_shape=pltpu.VMEM((64, 256), F32),
        scratch_shapes=[pltpu.VMEM((64, 1024), F32)],
        name="cross",
        compiler_params=SMALL,
    )(place, held(pieces), held(high), held(low))


def tail_kernel(
    me_ref, owners_ref, base_ref, second_hbm, mine_ref, other_ref, inverse_ref, panel_hbm, out_ref,
    cross_ref, second_ref, panel_ref, sem,
):
    fetch = pltpu.make_async_copy(second_hbm, second_ref, sem.at[8])
    copies = fetches(panel_hbm, panel_ref, sem, 0, 8)
    for copy in [fetch] + copies:
        copy.start()
    me = me_ref[0]
    core = me & 1
    for x in range(4):
        k = ((me >> 1) & 3) ^ x
        cross_ref[pl.ds(pl.multiple_of(128 * x + 64 * core, 64), 64), :] = mine_ref[k]
        cross_ref[pl.ds(pl.multiple_of(128 * x + 64 - 64 * core, 64), 64), :] = other_ref[k]

    def product(value, ref):
        return triple(*split(jnp.concatenate([value, turned(value)], 1)), ref)

    crossed = cross_ref[...].T
    fetch.wait()
    solved = product(second_ref[...] - crossed, inverse_ref)
    for copy in copies:
        copy.wait()
    update = base_ref[...] + jnp.where(owners_ref[0] == me, 0.0, product(solved, panel_ref))
    out_ref[...] = jnp.where(owners_ref[1] == me, -solved, update)


def tail(me, owners, base, second, mine, other, inverse, panel):
    return pl.pallas_call(
        tail_kernel,
        in_specs=[SMEM, SMEM, VMEM, HBM] + [VMEM] * 3 + [HBM],
        out_specs=VMEM,
        out_shape=pltpu.VMEM((256, 512), F32),
        scratch_shapes=[
            pltpu.VMEM((512, 256), F32),
            pltpu.VMEM((256, 512), F32),
            pltpu.VMEM((2, 512, 512), F32),
            pltpu.SemaphoreType.DMA((9,)),
        ],
        name="tail",
        compiler_params=SMALL,
    )(me, owners, held(base), in_hbm(second), held(mine), held(other), held(inverse), in_hbm(panel))


def half_kernel(me_ref, current_ref, out_ref):
    core = me_ref[0] & 1
    for j in range(16):
        out_ref[j] = current_ref[j, 1 - core]


def half(me, current):
    return pl.pallas_call(
        half_kernel,
        in_specs=[SMEM, VMEM],
        out_specs=VMEM,
        out_shape=pltpu.VMEM((16, 8, 512), F32),
        name="half",
        compiler_params=SMALL,
    )(me, held(current))


def combine_kernel(me_ref, owners_ref, current_ref, got_ref, update_ref, out_ref, stage_ref, sem):
    me = me_ref[0]
    core = me & 1
    later = (owners_ref[0] != me) & (owners_ref[1] != me)
    stores = []
    for j in range(16):
        own, got = current_ref[j, core], got_ref[j]
        for m in range(2):
            d = 2 * j + m
            value = jnp.where(later, jnp.where(core == m, own, got), 0.0) - update_ref[8 * d : 8 * d + 8, :]
            stage_ref[0, 4 * d : 4 * d + 4, :] = value[0:4]
            stage_ref[1, 4 * d : 4 * d + 4, :] = value[4:8]
        if j % 4 == 3:
            rows = pl.ds(8 * j - 24, 32)
            stores.append(pltpu.make_async_copy(stage_ref.at[:, rows], out_ref.at[:, rows], sem.at[j // 4]))
            stores[-1].start()
    for store in stores:
        store.wait()


def combine(me, owners, current, got, update):
    return pl.pallas_call(
        combine_kernel,
        in_specs=[SMEM, SMEM] + [VMEM] * 3,
        out_specs=HBM,
        out_shape=pltpu.HBM((2, 128, 512), F32),
        scratch_shapes=[pltpu.VMEM((2, 128, 512), F32), pltpu.SemaphoreType.DMA((4,))],
        name="combine",
        compiler_params=SMALL,
    )(me, owners, held(current), held(got), held(update))


ONE, TWO = 6, 12


def exchange(v, axis):
    return lax.all_to_all(v, axis, 0, 0, tiled=True)


def parts_of(v, axis):
    parts = [v]
    for k in range(1, 4):
        parts.append(lax.ppermute(v, axis, [(i, i ^ k) for i in range(4)]))
    return parts


def double(v, axis, k):
    other = lax.ppermute(v, axis, [(i, i ^ k) for i in range(4)])
    return jnp.stack([v, other])


def collect(v, axis):
    return jnp.stack(parts_of(v, axis))


def swap(v):
    return lax.ppermute(v, "c", [(0, 1), (1, 0)])


def shards(rhs_in, pivots, owners, panel_first, panel_second, inverse_first, inverse_second):
    row = ("z", "x", "c")
    me = lax.axis_index(row).astype(jnp.int32).reshape(1)
    place = lax.axis_index("y").astype(jnp.int32).reshape(1)
    rhs = rhs_in.reshape(2, 4, 128, 128).transpose(0, 2, 1, 3)
    piv = pivots.reshape(32, 1, 512)

    pieces = make_pieces(place, panel_first.reshape(2, 64, 8, 512))
    pieces = exchange(pieces, row[1:])
    left, gathered = head(rhs, piv, inverse_first)
    gathered = double(gathered, "z", 2)
    blocks = gather(owners, left, piv, 2, ONE)
    gathered = double(gathered, "x", 2)
    piece = pick(owners, pieces)
    parts = parts_of(piece, "z")
    blocks = gather(owners, left, piv, 2 + ONE, TWO, blocks)
    gathered = double(gathered, "z", 1)
    piece = choose(me, owners, parts)
    pieces = collect(piece, "y")
    gathered = double(gathered, "x", 1)
    blocks = gather(owners, left, piv, 2 + ONE + TWO, 30 - ONE - TWO, blocks)
    other = swap(gathered)
    current = exchange(blocks.reshape(16, 2, 8, 512), row[:2])
    high, low, solved, second = make_operands(me, gathered, other)
    crossed = cross(place, pieces, high, low)
    crossed = collect(crossed, "x")
    base = make_update(me, owners, high, low, solved, panel_first)
    send = half(me, current)
    got = swap(send)
    crossed_other = swap(crossed)
    update = tail(me, owners, base, second, crossed, crossed_other, inverse_second, panel_second)
    return combine(me, owners, current, got, update)


def solution(mesh):
    fine = Mesh(mesh.devices.reshape(4, 4, 2, 4, 2), ("z", "x", "c", "y", "h"))
    row = ("z", "x", "c")
    return jax.shard_map(
        shards,
        mesh=fine,
        in_specs=(
            P(None, ("y", "h") + row, None),
            P(),
            P(),
            P(None, row, None),
            P(None, row, None),
            P(),
            P(),
        ),
        out_specs=P(None, ("y", "h"), row),
        check_vma=False,
    )
```

time: 101 us -> 98.9 us (0.979)
  waiting for transfers between devices: 29.8 us -> 24.8 us
  Pallas kernels: 27.3 us -> 28.8 us
    ppermute x15 -> x13, waiting for transfers between devices: 29.8 us -> 24.8 us  [the longest x9 19.9 us: parts_of(): parts.append(lax.ppermute(v, axis, [(i, i ^ k) for i in range(4)]))]
    all_to_all x2, starting transfers between devices: 15.3 us -> 12.6 us  [exchange(): return lax.all_to_all(v, axis, 0, 0, tiled=True)]
    ppermute x15 -> x13, starting transfers between devices: 19.5 us -> 21.3 us  [the longest x9 11.9 us: parts_of(): parts.append(lax.ppermute(v, axis, [(i, i ^ k) for i in range(4)]))]
    ppermute x3, starting transfers between devices: 6.37 us -> 7.92 us  [swap(): return lax.ppermute(v, 'c', [(0, 1), (1, 0)])]
    unnamed x12 -> x10, local copies, waits for them, and re-layouts: 1.64 us -> 2.44 us
    pallas_call x3 -> x5, Pallas kernels: 8.64 us -> 9.42 us  [the longest x1 3.8 us: tail(): pl.pallas_call(tail_kernel, in_specs=[SMEM, SMEM, VMEM, HBM] + [VMEM] * 3...]
    pallas_call x2 -> x3, Pallas kernels: 13 us -> 13.4 us  [gather(): pl.pallas_call(functools.partial(gather_kernel, start, count), in_specs=s...]
  transfers between devices with their start and end apart: 20 -> 18, of which waited for: 8 -> 8; matrix products, arithmetic and copies ran while one was open for 0% -> 0% of each run, Pallas kernels for 22% -> 25%
where the time goes in v3:
time: 98.9 us; the launch traced here: 98.4 us
  starting transfers between devices  41.8 us (42%)
  Pallas kernels  28.8 us (29%)
  waiting for transfers between devices  24.8 us (25%)
  local copies, waits for them, and re-layouts  2.44 us (2%)
    ppermute x9, waiting for transfers between devices, parts_of(): parts.append(lax.ppermute(v, axis, [(i, i ^ k) for i in range(4)]))  19.9 us
    pallas_call x3, Pallas kernels, gather(): pl.pallas_call(functools.partial(gather_kernel, start, count), in_specs=s...  13.4 us
    all_to_all x2, starting transfers between devices, exchange(): return lax.all_to_all(v, axis, 0, 0, tiled=True)  12.6 us
    ppermute x9, starting transfers between devices, parts_of(): parts.append(lax.ppermute(v, axis, [(i, i ^ k) for i in range(4)]))  11.9 us
    ppermute x4, starting transfers between devices, double(): other = lax.ppermute(v, axis, [(i, i ^ k) for i in range(4)])  9.46 us
    ppermute x3, starting transfers between devices, swap(): return lax.ppermute(v, 'c', [(0, 1), (1, 0)])  7.92 us
    ppermute x4, waiting for transfers between devices, double(): other = lax.ppermute(v, axis, [(i, i ^ k) for i in range(4)])  4.97 us
    pallas_call x1, Pallas kernels, tail(): pl.pallas_call(tail_kernel, in_specs=[SMEM, SMEM, VMEM, HBM] + [VMEM] * 3...  3.8 us
  transfers between devices with their start and end apart: 18, of which 8 were waited for; matrix products, arithmetic and copies ran while one was open for 0% of the time, Pallas kernels for 25%

profile of v3, /device:TPU:1, one launch (start us, length us, event | category | flops | bytes accessed | tf_op | source)
XLA Modules:
  0.0 98.4 jit_solution(1399937672231725961)
XLA Ops:
  0.0 1.6 %copy-done = f32[2,512,512]{2,1,0:T(8,128)S(1)} copy-done((f32[2,512,512]{2,1,0:T(8,128)S(1)}, f32[2,512,512]{2,1,0:T(8,128)}, u32[]{:S(2)}) %copy-start) | copy-done | bytes 2097176
  1.6 0.8 copy-done.2
  2.4 2.7 %head.1 = (bf16[1024,256]{1,0:T(8,128)(2,1)S(1)}, f32[2,8,512]{2,1,0:T(8,128)S(1)}) custom-call(f32[2,128,4,128]{3,2,1,0:T(4,128)} %bitcast.40, s32[32,1,512]{2,1,0:T(1,128)S(1)} %bitcast.30, f32[2,512,512]{2,1,0:T(8,128)S(1)} %copy-done), custom_call_target="tpu_custom_call" | custom-call | tf_op jit(solution)/shard_map/head/pallas_call | solution.py:122
  5.2 3.9 %collective-permute-start.1 = (f32[2,8,512]{2,1,0:T(8,128)S(1)}, f32[2,8,512]{2,1,0:T(8,128)S(1)}, u32[]{:S(2)}, u32[]{:S(2)}) collective-permute-start(f32[2,8,512]{2,1,0:T(8,128)S(1)} %get-tuple-element.12), channel_id=1, source_target_pairs={{0,128},{64,192},{128,0},{192,64},{1,129},{65,193},{129,1},{193,65... | collective-permute-start | bytes 98312 | tf_op jit(solution)/shard_map/ppermute | solution.py:400
  9.1 1.3 %collective-permute-done.1 = f32[2,8,512]{2,1,0:T(8,128)S(1)} collective-permute-done((f32[2,8,512]{2,1,0:T(8,128)S(1)}, f32[2,8,512]{2,1,0:T(8,128)S(1)}, u32[]{:S(2)}, u32[]{:S(2)}) %collective-permute-start.1) | collective-permute-done | bytes 32800 | tf_op jit(solution)/shard_map/ppermute | solution.py:400
  10.4 2.8 %collective-permute-start.2 = (f32[2,2,8,512]{3,2,1,0:T(8,128)S(1)}, f32[2,2,8,512]{3,2,1,0:T(8,128)S(1)}, u32[]{:S(2)}, u32[]{:S(2)}) collective-permute-start(f32[2,2,8,512]{3,2,1,0:T(8,128)S(1)} %get-tuple-element.22), channel_id=1, source_target_pairs={{0,32},{16,48},{32,0},{48,16},{1,33},{17,49},{33,1},{49,17},{2,34}... | collective-permute-start | bytes 196616 | tf_op jit(solution)/shard_map/ppermute | solution.py:400
  13.2 1.9 %pieces.1 = f32[8,2,8,8,128]{4,3,2,1,0:T(8,128)} custom-call(s32[1]{0:T(128)} %bitcast.15.place_ref, f32[2,64,8,512]{3,2,1,0:T(8,128)} %bitcast.38), custom_call_target="tpu_custom_call" | custom-call | tf_op jit(solution)/shard_map/pieces/pallas_call | solution.py:84
  15.1 5.3 %all-to-all-start.1 = ((f32[8,2,8,8,128]{4,3,2,1,0:T(8,128)}), f32[8,2,8,8,128]{4,3,2,1,0:T(8,128)S(1)}, u32[]{:S(2)}, u32[]{:S(2)}) async-start(f32[8,2,8,8,128]{4,3,2,1,0:T(8,128)} %pieces.1), calls=%async_computation.1 | async-start | bytes 1048576 | tf_op jit(solution)/shard_map/all_to_all | solution.py:389
  20.4 0.0 collective-permute-done.2
  20.5 1.6 %collective-permute-start.3 = (f32[2,2,2,8,512]{4,3,2,1,0:T(8,128)S(1)}, f32[2,2,2,8,512]{4,3,2,1,0:T(8,128)S(1)}, u32[]{:S(2)}, u32[]{:S(2)}) collective-permute-start(f32[2,2,2,8,512]{4,3,2,1,0:T(8,128)S(1)} %get-tuple-element.20), channel_id=1, source_target_pairs={{0,64},{64,0},{128,192},{192,128},{1,65},{65,1},{129,193},{193,129... | collective-permute-start | bytes 393224 | tf_op jit(solution)/shard_map/ppermute | solution.py:400
  22.1 3.7 %collective-permute-done.3 = f32[2,2,2,8,512]{4,3,2,1,0:T(8,128)S(1)} collective-permute-done((f32[2,2,2,8,512]{4,3,2,1,0:T(8,128)S(1)}, f32[2,2,2,8,512]{4,3,2,1,0:T(8,128)S(1)}, u32[]{:S(2)}, u32[]{:S(2)}) %collective-permute-start.3) | collective-permute-done | bytes 131104 | tf_op jit(solution)/shard_map/ppermute | solution.py:400
  25.8 0.1 fusion.2
  25.8 1.1 %collective-permute-start.4 = (f32[2,2,2,2,8,512]{5,4,3,2,1,0:T(8,128)S(1)}, f32[2,2,2,2,8,512]{5,4,3,2,1,0:T(8,128)S(1)}, u32[]{:S(2)}, u32[]{:S(2)}) collective-permute-start(f32[2,2,2,2,8,512]{5,4,3,2,1,0:T(8,128)S(1)} %get-tuple-element.18), channel_id=1, source_target_pairs={{0,16},{16,0},{32,48},{48,32},{1,17},{17,1},{33,49},{49,33},{2,18}... | collective-permute-start | bytes 786440 | tf_op jit(solution)/shard_map/ppermute | solution.py:400
  26.9 3.1 %gather_blocks.3.rest_0_ = f32[32,8,512]{2,1,0:T(8,128)} custom-call(s32[32]{0:T(128)S(1)} %copy-done.4, bf16[1024,256]{1,0:T(8,128)(2,1)S(1)} %get-tuple-element.11.left_ref, s32[32,1,512]{2,1,0:T(1,128)S(1)} %bitcast.31), custom_call_target="tpu_custom_call" | custom-call | tf_op jit(solution)/shard_map/gather_blocks/pallas_call | solution.py:160
  30.0 5.1 %gather_blocks.4.rest_0_ = f32[32,8,512]{2,1,0:T(8,128)} custom-call(s32[32]{0:T(128)S(1)} %copy-done.4, bf16[1024,256]{1,0:T(8,128)(2,1)S(1)} %get-tuple-element.11.left_ref, s32[32,1,512]{2,1,0:T(1,128)S(1)} %bitcast.32, f32[32,8,512]{2,1,0:T(8,128)} %gather_blocks.3.rest_0_), custom_call_target="tpu_custom_call", output_to_operand_aliasing={{}: (3, {})} | custom-call | tf_op jit(solution)/shard_map/gather_blocks/pallas_call | solution.py:160
  35.2 5.1 %gather_blocks.5 = f32[32,8,512]{2,1,0:T(8,128)} custom-call(s32[32]{0:T(128)S(1)} %copy-done.4, bf16[1024,256]{1,0:T(8,128)(2,1)S(1)} %get-tuple-element.11.left_ref, s32[32,1,512]{2,1,0:T(1,128)S(1)} %bitcast.33, f32[32,8,512]{2,1,0:T(8,128)} %gather_blocks.4.rest_0_), custom_call_target="tpu_custom_call", output_to_operand_aliasing={{}: (3, {})} | custom-call | tf_op jit(solution)/shard_map/gather_blocks/pallas_call | solution.py:160
  40.3 0.0 all-to-all-done.1.all_ref
  40.3 7.2 %all-to-all-start = ((f32[16,2,8,512]{3,2,1,0:T(8,128)}), f32[16,2,8,512]{3,2,1,0:T(8,128)S(1)}, u32[]{:S(2)}, u32[]{:S(2)}) async-start(f32[16,2,8,512]{3,2,1,0:T(8,128)} %bitcast.39), calls=%async_computation | async-start | bytes 1048576 | tf_op jit(solution)/shard_map/all_to_all | solution.py:389
  47.6 0.0 collective-permute-done.4
  47.6 1.9 %collective-permute-start.5 = (f32[2,2,2,2,2,8,512]{6,5,4,3,2,1,0:T(8,128)S(1)}, f32[2,2,2,2,2,8,512]{6,5,4,3,2,1,0:T(8,128)S(1)}, u32[]{:S(2)}, u32[]{:S(2)}) collective-permute-start(f32[2,2,2,2,2,8,512]{6,5,4,3,2,1,0:T(8,128)S(1)} %pad_maximum_fusion), channel_id=1, source_target_pairs={{0,8},{8,0},{1,9},{9,1},{2,10},{10,2},{3,11},{11,3},{4,12},{12,4},... | collective-permute-start | bytes 1572872 | tf_op jit(solution)/shard_map/ppermute | solution.py:409
  49.5 0.5 pick.1.own_ref
  50.1 1.7 %collective-permute-start.6 = (f32[2,8,8,128]{3,2,1,0:T(8,128)S(1)}, f32[2,8,8,128]{3,2,1,0:T(8,128)S(1)}, u32[]{:S(2)}, u32[]{:S(2)}) collective-permute-start(f32[2,8,8,128]{3,2,1,0:T(8,128)S(1)} %pick.1.own_ref), channel_id=1, source_target_pairs={{0,64},{64,0},{128,192},{192,128},{1,65},{65,1},{129,193},{193,129... | collective-permute-start | bytes 196616 | tf_op jit(solution)/shard_map/ppermute | solution.py:395
  51.8 2.1 %collective-permute-start.7 = (f32[2,8,8,128]{3,2,1,0:T(8,128)S(1)}, f32[2,8,8,128]{3,2,1,0:T(8,128)S(1)}, u32[]{:S(2)}, u32[]{:S(2)}) collective-permute-start(f32[2,8,8,128]{3,2,1,0:T(8,128)S(1)} %pick.1.own_ref), channel_id=1, source_target_pairs={{0,128},{64,192},{128,0},{192,64},{1,129},{65,193},{129,1},{193,65... | collective-permute-start | bytes 196616 | tf_op jit(solution)/shard_map/ppermute | solution.py:395
  53.9 0.1 collective-permute-start.8
  54.0 2.6 %collective-permute-done.6.one_ref = f32[2,8,8,128]{3,2,1,0:T(8,128)S(1)} collective-permute-done((f32[2,8,8,128]{3,2,1,0:T(8,128)S(1)}, f32[2,8,8,128]{3,2,1,0:T(8,128)S(1)}, u32[]{:S(2)}, u32[]{:S(2)}) %collective-permute-start.6) | collective-permute-done | bytes 65568 | tf_op jit(solution)/shard_map/ppermute | solution.py:395
  56.6 8.9 %collective-permute-done.7.two_ref = f32[2,8,8,128]{3,2,1,0:T(8,128)S(1)} collective-permute-done((f32[2,8,8,128]{3,2,1,0:T(8,128)S(1)}, f32[2,8,8,128]{3,2,1,0:T(8,128)S(1)}, u32[]{:S(2)}, u32[]{:S(2)}) %collective-permute-start.7) | collective-permute-done | bytes 65568 | tf_op jit(solution)/shard_map/ppermute | solution.py:395
  65.4 0.0 collective-permute-done.8.three_ref
  65.4 0.6 choose.1
  66.0 1.4 %collective-permute-start.9 = (f32[2,8,8,128]{3,2,1,0:T(8,128)S(1)}, f32[2,8,8,128]{3,2,1,0:T(8,128)S(1)}, u32[]{:S(2)}, u32[]{:S(2)}) collective-permute-start(f32[2,8,8,128]{3,2,1,0:T(8,128)S(1)} %choose.1), channel_id=1, source_target_pairs={{0,2},{2,0},{4,6},{6,4},{1,3},{3,1},{5,7},{7,5},{8,10},{10,8},{12,... | collective-permute-start | bytes 196616 | tf_op jit(solution)/shard_map/ppermute | solution.py:395
  67.4 2.6 %collective-permute-start.10 = (f32[2,8,8,128]{3,2,1,0:T(8,128)S(1)}, f32[2,8,8,128]{3,2,1,0:T(8,128)S(1)}, u32[]{:S(2)}, u32[]{:S(2)}) collective-permute-start(f32[2,8,8,128]{3,2,1,0:T(8,128)S(1)} %choose.1), channel_id=1, source_target_pairs={{0,4},{2,6},{4,0},{6,2},{1,5},{3,7},{5,1},{7,3},{8,12},{10,14},{12... | collective-permute-start | bytes 196616 | tf_op jit(solution)/shard_map/ppermute | solution.py:395
  70.0 0.0 collective-permute-start.11
  70.0 0.0 collective-permute-done.9
  70.0 2.3 %collective-permute-done.10 = f32[2,8,8,128]{3,2,1,0:T(8,128)S(1)} collective-permute-done((f32[2,8,8,128]{3,2,1,0:T(8,128)S(1)}, f32[2,8,8,128]{3,2,1,0:T(8,128)S(1)}, u32[]{:S(2)}, u32[]{:S(2)}) %collective-permute-start.10) | collective-permute-done | bytes 65568 | tf_op jit(solution)/shard_map/ppermute | solution.py:395
  72.4 2.0 %collective-permute-done.11 = f32[2,8,8,128]{3,2,1,0:T(8,128)S(1)} collective-permute-done((f32[2,8,8,128]{3,2,1,0:T(8,128)S(1)}, f32[2,8,8,128]{3,2,1,0:T(8,128)S(1)}, u32[]{:S(2)}, u32[]{:S(2)}) %collective-permute-start.11) | collective-permute-done | bytes 65568 | tf_op jit(solution)/shard_map/ppermute | solution.py:395
  74.4 0.9 operands.1
  75.3 0.5 cross.1
  75.7 1.3 %collective-permute-start.12 = (f32[64,256]{1,0:T(8,128)S(1)}, f32[64,256]{1,0:T(8,128)S(1)}, u32[]{:S(2)}, u32[]{:S(2)}) collective-permute-start(f32[64,256]{1,0:T(8,128)S(1)} %cross.1), channel_id=1, source_target_pairs={{0,16},{16,0},{32,48},{48,32},{1,17},{17,1},{33,49},{49,33},{2,18}... | collective-permute-start | bytes 196616 | tf_op jit(solution)/shard_map/ppermute | solution.py:395
  77.0 2.4 %collective-permute-start.13 = (f32[64,256]{1,0:T(8,128)S(1)}, f32[64,256]{1,0:T(8,128)S(1)}, u32[]{:S(2)}, u32[]{:S(2)}) collective-permute-start(f32[64,256]{1,0:T(8,128)S(1)} %cross.1), channel_id=1, source_target_pairs={{0,32},{16,48},{32,0},{48,16},{1,33},{17,49},{33,1},{49,17},{2,34}... | collective-permute-start | bytes 196616 | tf_op jit(solution)/shard_map/ppermute | solution.py:395
  79.4 0.2 collective-permute-start.14
  79.7 2.1 %collective-permute-done.13 = f32[64,256]{1,0:T(8,128)S(1)} collective-permute-done((f32[64,256]{1,0:T(8,128)S(1)}, f32[64,256]{1,0:T(8,128)S(1)}, u32[]{:S(2)}, u32[]{:S(2)}) %collective-permute-start.13) | collective-permute-done | bytes 65568 | tf_op jit(solution)/shard_map/ppermute | solution.py:395
  81.8 2.0 %collective-permute-done.14 = f32[64,256]{1,0:T(8,128)S(1)} collective-permute-done((f32[64,256]{1,0:T(8,128)S(1)}, f32[64,256]{1,0:T(8,128)S(1)}, u32[]{:S(2)}, u32[]{:S(2)}) %collective-permute-start.14) | collective-permute-done | bytes 65568 | tf_op jit(solution)/shard_map/ppermute | solution.py:395
  83.8 5.9 %collective-permute-start.15 = (f32[4,64,256]{2,1,0:T(8,128)S(1)}, f32[4,64,256]{2,1,0:T(8,128)S(1)}, u32[]{:S(2)}, u32[]{:S(2)}) collective-permute-start(f32[4,64,256]{2,1,0:T(8,128)S(1)} %pad_maximum_fusion.3.mine_ref), channel_id=1, source_target_pairs={{0,8},{8,0},{1,9},{9,1},{2,10},{10,2},{3,11},{11,3},{4,12},{12,4},... | collective-permute-start | bytes 786440 | tf_op jit(solution)/shard_map/ppermute | solution.py:409
  89.7 0.0 all-to-all-done.current_ref
  89.7 0.1 collective-permute-start
  89.8 3.2 %update.1.base_ref = f32[256,512]{1,0:T(8,128)S(1)} custom-call(s32[1]{0:T(128)} %bitcast.me_ref, s32[32]{0:T(128)S(1)} %copy-done.4, bf16[256,1024]{1,0:T(8,128)(2,1)S(1)} %get-tuple-element.13.high_ref, bf16[256,1024]{1,0:T(8,128)(2,1)S(1)} %get-tuple-element.14.low_ref, f32[256,512]{1,0:T(8,128)S(1)} %get-tuple-element.15.solved_ref, f32[2,512,512]{2,1,0:T(8,128)} %panel_hbm.2), custom_call_target="tpu_custom_call" | custom-call | tf_op jit(solution)/shard_map/update/pallas_call | solution.py:259
  93.1 3.8 %tail.1.update_ref = f32[256,512]{1,0:T(8,128)S(1)} custom-call(s32[1]{0:T(128)} %bitcast.me_ref, s32[32]{0:T(128)S(1)} %copy-done.4, f32[256,512]{1,0:T(8,128)S(1)} %update.1.base_ref, f32[256,512]{1,0:T(8,128)} %get-tuple-element.16.second_hbm, f32[4,64,256]{2,1,0:T(8,128)S(1)} %pad_maximum_fusion.3.mine_ref, ...), custom_call_target="tpu_custom_call" | custom-call | tf_op jit(solution)/shard_map/tail/pallas_call | solution.py:320
  96.9 0.0 collective-permute-done.got_ref
  96.9 1.4 %combine.1 = f32[2,128,512]{2,1,0:T(8,128)} custom-call(s32[1]{0:T(128)} %bitcast.me_ref, s32[32]{0:T(128)S(1)} %copy-done.4, f32[16,2,8,512]{3,2,1,0:T(8,128)S(1)} %all-to-all-done.current_ref, f32[16,8,512]{2,1,0:T(8,128)S(1)} %collective-permute-done.got_ref, f32[256,512]{1,0:T(8,128)S(1)} %tail.1.update_ref), custom_call_target="tpu_custom_call" | custom-call | tf_op jit(solution)/shard_map/combine/pallas_call | solution.py:374
  (17 shorter events, 0.1 us)
Async XLA Ops:
  0.0 1.6 %copy-start = (f32[2,512,512]{2,1,0:T(8,128)S(1)}, f32[2,512,512]{2,1,0:T(8,128)}, u32[]{:S(2)}) copy-start(f32[2,512,512]{2,1,0:T(8,128)} %inverse_ref.2) | copy-start | bytes 6291460
  1.6 0.8 copy-start.2
  5.2 5.2 %collective-permute-start.1 = (f32[2,8,512]{2,1,0:T(8,128)S(1)}, f32[2,8,512]{2,1,0:T(8,128)S(1)}, u32[]{:S(2)}, u32[]{:S(2)}) collective-permute-start(f32[2,8,512]{2,1,0:T(8,128)S(1)} %get-tuple-element.12), channel_id=1, source_target_pairs={{0,128},{64,192},{128,0},{192,64},{1,129},{65,193},{129,1},{193,65... | collective-permute-start | bytes 98312 | tf_op jit(solution)/shard_map/ppermute | solution.py:400
  10.4 10.0 %collective-permute-start.2 = (f32[2,2,8,512]{3,2,1,0:T(8,128)S(1)}, f32[2,2,8,512]{3,2,1,0:T(8,128)S(1)}, u32[]{:S(2)}, u32[]{:S(2)}) collective-permute-start(f32[2,2,8,512]{3,2,1,0:T(8,128)S(1)} %get-tuple-element.22), channel_id=1, source_target_pairs={{0,32},{16,48},{32,0},{48,16},{1,33},{17,49},{33,1},{49,17},{2,34}... | collective-permute-start | bytes 196616 | tf_op jit(solution)/shard_map/ppermute | solution.py:400
  13.2 13.7 %copy-start.3 = (s32[16384]{0:T(1024)S(1)}, s32[16384]{0:T(1024)}, u32[]{:S(2)}) copy-start(s32[16384]{0:T(1024)} %param.8) | copy-start | bytes 196612
  13.2 13.7 %copy-start.4 = (s32[32]{0:T(128)S(1)}, s32[32]{0:T(128)}, u32[]{:S(2)}) copy-start(s32[32]{0:T(128)} %owners_ref.15) | copy-start | bytes 388
  15.1 25.2 %all-to-all-start.1 = ((f32[8,2,8,8,128]{4,3,2,1,0:T(8,128)}), f32[8,2,8,8,128]{4,3,2,1,0:T(8,128)S(1)}, u32[]{:S(2)}, u32[]{:S(2)}) async-start(f32[8,2,8,8,128]{4,3,2,1,0:T(8,128)} %pieces.1), calls=%async_computation.1 | async-start | bytes 1048576 | tf_op jit(solution)/shard_map/all_to_all | solution.py:389
  20.5 5.3 %collective-permute-start.3 = (f32[2,2,2,8,512]{4,3,2,1,0:T(8,128)S(1)}, f32[2,2,2,8,512]{4,3,2,1,0:T(8,128)S(1)}, u32[]{:S(2)}, u32[]{:S(2)}) collective-permute-start(f32[2,2,2,8,512]{4,3,2,1,0:T(8,128)S(1)} %get-tuple-element.20), channel_id=1, source_target_pairs={{0,64},{64,0},{128,192},{192,128},{1,65},{65,1},{129,193},{193,129... | collective-permute-start | bytes 393224 | tf_op jit(solution)/shard_map/ppermute | solution.py:400
  25.8 21.8 %collective-permute-start.4 = (f32[2,2,2,2,8,512]{5,4,3,2,1,0:T(8,128)S(1)}, f32[2,2,2,2,8,512]{5,4,3,2,1,0:T(8,128)S(1)}, u32[]{:S(2)}, u32[]{:S(2)}) collective-permute-start(f32[2,2,2,2,8,512]{5,4,3,2,1,0:T(8,128)S(1)} %get-tuple-element.18), channel_id=1, source_target_pairs={{0,16},{16,0},{32,48},{48,32},{1,17},{17,1},{33,49},{49,33},{2,18}... | collective-permute-start | bytes 786440 | tf_op jit(solution)/shard_map/ppermute | solution.py:400
  40.3 49.4 %all-to-all-start = ((f32[16,2,8,512]{3,2,1,0:T(8,128)}), f32[16,2,8,512]{3,2,1,0:T(8,128)S(1)}, u32[]{:S(2)}, u32[]{:S(2)}) async-start(f32[16,2,8,512]{3,2,1,0:T(8,128)} %bitcast.39), calls=%async_computation | async-start | bytes 1048576 | tf_op jit(solution)/shard_map/all_to_all | solution.py:389
  47.6 26.7 %collective-permute-start.5 = (f32[2,2,2,2,2,8,512]{6,5,4,3,2,1,0:T(8,128)S(1)}, f32[2,2,2,2,2,8,512]{6,5,4,3,2,1,0:T(8,128)S(1)}, u32[]{:S(2)}, u32[]{:S(2)}) collective-permute-start(f32[2,2,2,2,2,8,512]{6,5,4,3,2,1,0:T(8,128)S(1)} %pad_maximum_fusion), channel_id=1, source_target_pairs={{0,8},{8,0},{1,9},{9,1},{2,10},{10,2},{3,11},{11,3},{4,12},{12,4},... | collective-permute-start | bytes 1572872 | tf_op jit(solution)/shard_map/ppermute | solution.py:409
  50.1 6.5 %collective-permute-start.6 = (f32[2,8,8,128]{3,2,1,0:T(8,128)S(1)}, f32[2,8,8,128]{3,2,1,0:T(8,128)S(1)}, u32[]{:S(2)}, u32[]{:S(2)}) collective-permute-start(f32[2,8,8,128]{3,2,1,0:T(8,128)S(1)} %pick.1.own_ref), channel_id=1, source_target_pairs={{0,64},{64,0},{128,192},{192,128},{1,65},{65,1},{129,193},{193,129... | collective-permute-start | bytes 196616 | tf_op jit(solution)/shard_map/ppermute | solution.py:395
  51.8 13.6 %collective-permute-start.7 = (f32[2,8,8,128]{3,2,1,0:T(8,128)S(1)}, f32[2,8,8,128]{3,2,1,0:T(8,128)S(1)}, u32[]{:S(2)}, u32[]{:S(2)}) collective-permute-start(f32[2,8,8,128]{3,2,1,0:T(8,128)S(1)} %pick.1.own_ref), channel_id=1, source_target_pairs={{0,128},{64,192},{128,0},{192,64},{1,129},{65,193},{129,1},{193,65... | collective-permute-start | bytes 196616 | tf_op jit(solution)/shard_map/ppermute | solution.py:395
  53.9 11.5 %collective-permute-start.8 = (f32[2,8,8,128]{3,2,1,0:T(8,128)S(1)}, f32[2,8,8,128]{3,2,1,0:T(8,128)S(1)}, u32[]{:S(2)}, u32[]{:S(2)}) collective-permute-start(f32[2,8,8,128]{3,2,1,0:T(8,128)S(1)} %pick.1.own_ref), channel_id=1, source_target_pairs={{0,192},{64,128},{128,64},{192,0},{1,193},{65,129},{129,65},{193,1... | collective-permute-start | bytes 196616 | tf_op jit(solution)/shard_map/ppermute | solution.py:395
  66.0 4.0 %collective-permute-start.9 = (f32[2,8,8,128]{3,2,1,0:T(8,128)S(1)}, f32[2,8,8,128]{3,2,1,0:T(8,128)S(1)}, u32[]{:S(2)}, u32[]{:S(2)}) collective-permute-start(f32[2,8,8,128]{3,2,1,0:T(8,128)S(1)} %choose.1), channel_id=1, source_target_pairs={{0,2},{2,0},{4,6},{6,4},{1,3},{3,1},{5,7},{7,5},{8,10},{10,8},{12,... | collective-permute-start | bytes 196616 | tf_op jit(solution)/shard_map/ppermute | solution.py:395
  67.4 5.0 %collective-permute-start.10 = (f32[2,8,8,128]{3,2,1,0:T(8,128)S(1)}, f32[2,8,8,128]{3,2,1,0:T(8,128)S(1)}, u32[]{:S(2)}, u32[]{:S(2)}) collective-permute-start(f32[2,8,8,128]{3,2,1,0:T(8,128)S(1)} %choose.1), channel_id=1, source_target_pairs={{0,4},{2,6},{4,0},{6,2},{1,5},{3,7},{5,1},{7,3},{8,12},{10,14},{12... | collective-permute-start | bytes 196616 | tf_op jit(solution)/shard_map/ppermute | solution.py:395
  70.0 4.3 %collective-permute-start.11 = (f32[2,8,8,128]{3,2,1,0:T(8,128)S(1)}, f32[2,8,8,128]{3,2,1,0:T(8,128)S(1)}, u32[]{:S(2)}, u32[]{:S(2)}) collective-permute-start(f32[2,8,8,128]{3,2,1,0:T(8,128)S(1)} %choose.1), channel_id=1, source_target_pairs={{0,6},{2,4},{4,2},{6,0},{1,7},{3,5},{5,3},{7,1},{8,14},{10,12},{12... | collective-permute-start | bytes 196616 | tf_op jit(solution)/shard_map/ppermute | solution.py:395
  75.7 3.9 %collective-permute-start.12 = (f32[64,256]{1,0:T(8,128)S(1)}, f32[64,256]{1,0:T(8,128)S(1)}, u32[]{:S(2)}, u32[]{:S(2)}) collective-permute-start(f32[64,256]{1,0:T(8,128)S(1)} %cross.1), channel_id=1, source_target_pairs={{0,16},{16,0},{32,48},{48,32},{1,17},{17,1},{33,49},{49,33},{2,18}... | collective-permute-start | bytes 196616 | tf_op jit(solution)/shard_map/ppermute | solution.py:395
  77.0 4.8 %collective-permute-start.13 = (f32[64,256]{1,0:T(8,128)S(1)}, f32[64,256]{1,0:T(8,128)S(1)}, u32[]{:S(2)}, u32[]{:S(2)}) collective-permute-start(f32[64,256]{1,0:T(8,128)S(1)} %cross.1), channel_id=1, source_target_pairs={{0,32},{16,48},{32,0},{48,16},{1,33},{17,49},{33,1},{49,17},{2,34}... | collective-permute-start | bytes 196616 | tf_op jit(solution)/shard_map/ppermute | solution.py:395
  79.4 4.3 %collective-permute-start.14 = (f32[64,256]{1,0:T(8,128)S(1)}, f32[64,256]{1,0:T(8,128)S(1)}, u32[]{:S(2)}, u32[]{:S(2)}) collective-permute-start(f32[64,256]{1,0:T(8,128)S(1)} %cross.1), channel_id=1, source_target_pairs={{0,48},{16,32},{32,16},{48,0},{1,49},{17,33},{33,17},{49,1},{2,50}... | collective-permute-start | bytes 196616 | tf_op jit(solution)/shard_map/ppermute | solution.py:395
  83.8 9.3 %collective-permute-start.15 = (f32[4,64,256]{2,1,0:T(8,128)S(1)}, f32[4,64,256]{2,1,0:T(8,128)S(1)}, u32[]{:S(2)}, u32[]{:S(2)}) collective-permute-start(f32[4,64,256]{2,1,0:T(8,128)S(1)} %pad_maximum_fusion.3.mine_ref), channel_id=1, source_target_pairs={{0,8},{8,0},{1,9},{9,1},{2,10},{10,2},{3,11},{11,3},{4,12},{12,4},... | collective-permute-start | bytes 786440 | tf_op jit(solution)/shard_map/ppermute | solution.py:409
  89.7 7.2 %collective-permute-start = (f32[16,8,512]{2,1,0:T(8,128)S(1)}, f32[16,8,512]{2,1,0:T(8,128)S(1)}, u32[]{:S(2)}, u32[]{:S(2)}) collective-permute-start(f32[16,8,512]{2,1,0:T(8,128)S(1)} %half.1), channel_id=1, source_target_pairs={{0,8},{8,0},{1,9},{9,1},{2,10},{10,2},{3,11},{11,3},{4,12},{12,4},... | collective-permute-start | bytes 786440 | tf_op jit(solution)/shard_map/ppermute | solution.py:409
  89.8 3.2 %copy-start.1 = (f32[2,512,512]{2,1,0:T(8,128)S(1)}, f32[2,512,512]{2,1,0:T(8,128)}, u32[]{:S(2)}) copy-start(f32[2,512,512]{2,1,0:T(8,128)} %inverse_ref.3) | copy-start | bytes 6291460

commit v4 on v3

--- a/solution.py
+++ b/solution.py
@@ -144,7 +144,7 @@
         send(i).start()
         return carry
 
-    lax.fori_loop(0, count, step, 0, unroll=6)
+    lax.fori_loop(0, count, step, 0, unroll=min(count, 12))
     for i in range(count):
         send(i).wait()
 
@@ -333,53 +333,32 @@
     )(me, owners, held(base), in_hbm(second), held(mine), held(other), held(inverse), in_hbm(panel))
 
 
-def half_kernel(me_ref, current_ref, out_ref):
-    core = me_ref[0] & 1
-    for j in range(16):
-        out_ref[j] = current_ref[j, 1 - core]
-
-
-def half(me, current):
-    return pl.pallas_call(
-        half_kernel,
-        in_specs=[SMEM, VMEM],
-        out_specs=VMEM,
-        out_shape=pltpu.VMEM((16, 8, 512), F32),
-        name="half",
-        compiler_params=SMALL,
-    )(me, held(current))
-
-
-def combine_kernel(me_ref, owners_ref, current_ref, got_ref, update_ref, out_ref, stage_ref, sem):
+def combine_kernel(me_ref, owners_ref, current_ref, update_ref, out_ref, stage_ref, sem):
     me = me_ref[0]
-    core = me & 1
     later = (owners_ref[0] != me) & (owners_ref[1] != me)
     stores = []
-    for j in range(16):
-        own, got = current_ref[j, core], got_ref[j]
-        for m in range(2):
-            d = 2 * j + m
-            value = jnp.where(later, jnp.where(core == m, own, got), 0.0) - update_ref[8 * d : 8 * d + 8, :]
-            stage_ref[0, 4 * d : 4 * d + 4, :] = value[0:4]
-            stage_ref[1, 4 * d : 4 * d + 4, :] = value[4:8]
-        if j % 4 == 3:
-            rows = pl.ds(8 * j - 24, 32)
-            stores.append(pltpu.make_async_copy(stage_ref.at[:, rows], out_ref.at[:, rows], sem.at[j // 4]))
+    for d in range(32):
+        value = jnp.where(later, current_ref[d], 0.0) - update_ref[8 * d : 8 * d + 8, :]
+        stage_ref[0, 4 * d : 4 * d + 4, :] = value[0:4]
+        stage_ref[1, 4 * d : 4 * d + 4, :] = value[4:8]
+        if d % 8 == 7:
+            rows = pl.ds(4 * d - 28, 32)
+            stores.append(pltpu.make_async_copy(stage_ref.at[:, rows], out_ref.at[:, rows], sem.at[d // 8]))
             stores[-1].start()
     for store in stores:
         store.wait()
 
 
-def combine(me, owners, current, got, update):
+def combine(me, owners, current, update):
     return pl.pallas_call(
         combine_kernel,
-        in_specs=[SMEM, SMEM] + [VMEM] * 3,
+        in_specs=[SMEM, SMEM] + [VMEM] * 2,
         out_specs=HBM,
         out_shape=pltpu.HBM((2, 128, 512), F32),
         scratch_shapes=[pltpu.VMEM((2, 128, 512), F32), pltpu.SemaphoreType.DMA((4,))],
         name="combine",
         compiler_params=SMALL,
-    )(me, owners, held(current), held(got), held(update))
+    )(me, owners, held(current), held(update))
 
 
 ONE, TWO = 6, 12
@@ -431,16 +410,14 @@
     gathered = double(gathered, "x", 1)
     blocks = gather(owners, left, piv, 2 + ONE + TWO, 30 - ONE - TWO, blocks)
     other = swap(gathered)
-    current = exchange(blocks.reshape(16, 2, 8, 512), row[:2])
+    current = exchange(blocks, row)
     high, low, solved, second = make_operands(me, gathered, other)
     crossed = cross(place, pieces, high, low)
     crossed = collect(crossed, "x")
     base = make_update(me, owners, high, low, solved, panel_first)
-    send = half(me, current)
-    got = swap(send)
     crossed_other = swap(crossed)
     update = tail(me, owners, base, second, crossed, crossed_other, inverse_second, panel_second)
-    return combine(me, owners, current, got, update)
+    return combine(me, owners, current, update)
 
 
 def solution(mesh):

time: 98.9 us -> 96.8 us (0.979)
  starting transfers between devices: 41.8 us -> 40.1 us
    ppermute x3 -> x2, starting transfers between devices: 7.92 us -> 4.8 us  [swap(): return lax.ppermute(v, 'c', [(0, 1), (1, 0)])]
    all_to_all x2, starting transfers between devices: 12.6 us -> 14.4 us  [exchange(): return lax.all_to_all(v, axis, 0, 0, tiled=True)]
    ppermute x4, waiting for transfers between devices: 4.97 us -> 3.19 us  [double(): other = lax.ppermute(v, axis, [(i, i ^ k) for i in range(4)])]
    ppermute x9, waiting for transfers between devices: 19.9 us -> 21.5 us  [parts_of(): parts.append(lax.ppermute(v, axis, [(i, i ^ k) for i in range(4)]))]
    ppermute x9, starting transfers between devices: 11.9 us -> 10.8 us  [parts_of(): parts.append(lax.ppermute(v, axis, [(i, i ^ k) for i in range(4)]))]
  transfers between devices with their start and end apart: 18 -> 17, of which waited for: 8 -> 8; matrix products, arithmetic and copies ran while one was open for 0% -> 0% of each run, Pallas kernels for 25% -> 25%
where the time goes in v4:
time: 96.8 us; the launch traced here: 96.3 us
  starting transfers between devices  40.1 us (41%)
  Pallas kernels  28.5 us (29%)
  waiting for transfers between devices  24.7 us (26%)
  local copies, waits for them, and re-layouts  2.44 us (3%)
    ppermute x9, waiting for transfers between devices, parts_of(): parts.append(lax.ppermute(v, axis, [(i, i ^ k) for i in range(4)]))  21.5 us
    all_to_all x2, starting transfers between devices, exchange(): return lax.all_to_all(v, axis, 0, 0, tiled=True)  14.4 us
    pallas_call x3, Pallas kernels, gather(): pl.pallas_call(functools.partial(gather_kernel, start, count), in_specs=s...  13.1 us
    ppermute x9, starting transfers between devices, parts_of(): parts.append(lax.ppermute(v, axis, [(i, i ^ k) for i in range(4)]))  10.8 us
    ppermute x4, starting transfers between devices, double(): other = lax.ppermute(v, axis, [(i, i ^ k) for i in range(4)])  10.1 us
    ppermute x2, starting transfers between devices, swap(): return lax.ppermute(v, 'c', [(0, 1), (1, 0)])  4.8 us
    pallas_call x1, Pallas kernels, tail(): pl.pallas_call(tail_kernel, in_specs=[SMEM, SMEM, VMEM, HBM] + [VMEM] * 3...  3.79 us
    pallas_call x1, Pallas kernels, make_update(): pl.pallas_call(update_kernel, in_specs=[SMEM, SMEM, VMEM, VMEM, VMEM, HBM...  3.23 us
  transfers between devices with their start and end apart: 17, of which 8 were waited for; matrix products, arithmetic and copies ran while one was open for 0% of the time, Pallas kernels for 25%

profile of v4, /device:TPU:1, one launch (start us, length us, event | category | flops | bytes accessed | tf_op | source)
XLA Modules:
  0.0 96.3 jit_solution(5817135948220087760)
XLA Ops:
  0.0 1.6 %copy-done = f32[2,512,512]{2,1,0:T(8,128)S(1)} copy-done((f32[2,512,512]{2,1,0:T(8,128)S(1)}, f32[2,512,512]{2,1,0:T(8,128)}, u32[]{:S(2)}) %copy-start) | copy-done | bytes 2097176
  1.6 0.8 copy-done.2
  2.4 2.7 %head.1 = (bf16[1024,256]{1,0:T(8,128)(2,1)S(1)}, f32[2,8,512]{2,1,0:T(8,128)S(1)}) custom-call(f32[2,128,4,128]{3,2,1,0:T(4,128)} %bitcast.38, s32[32,1,512]{2,1,0:T(1,128)S(1)} %bitcast.29, f32[2,512,512]{2,1,0:T(8,128)S(1)} %copy-done), custom_call_target="tpu_custom_call" | custom-call | tf_op jit(solution)/shard_map/head/pallas_call | solution.py:122
  5.2 3.9 %collective-permute-start = (f32[2,8,512]{2,1,0:T(8,128)S(1)}, f32[2,8,512]{2,1,0:T(8,128)S(1)}, u32[]{:S(2)}, u32[]{:S(2)}) collective-permute-start(f32[2,8,512]{2,1,0:T(8,128)S(1)} %get-tuple-element.12), channel_id=1, source_target_pairs={{0,128},{64,192},{128,0},{192,64},{1,129},{65,193},{129,1},{193,65... | collective-permute-start | bytes 98312 | tf_op jit(solution)/shard_map/ppermute | solution.py:379
  9.1 1.3 %collective-permute-done = f32[2,8,512]{2,1,0:T(8,128)S(1)} collective-permute-done((f32[2,8,512]{2,1,0:T(8,128)S(1)}, f32[2,8,512]{2,1,0:T(8,128)S(1)}, u32[]{:S(2)}, u32[]{:S(2)}) %collective-permute-start) | collective-permute-done | bytes 32800 | tf_op jit(solution)/shard_map/ppermute | solution.py:379
  10.4 2.8 %collective-permute-start.1 = (f32[2,2,8,512]{3,2,1,0:T(8,128)S(1)}, f32[2,2,8,512]{3,2,1,0:T(8,128)S(1)}, u32[]{:S(2)}, u32[]{:S(2)}) collective-permute-start(f32[2,2,8,512]{3,2,1,0:T(8,128)S(1)} %get-tuple-element.22), channel_id=1, source_target_pairs={{0,32},{16,48},{32,0},{48,16},{1,33},{17,49},{33,1},{49,17},{2,34}... | collective-permute-start | bytes 196616 | tf_op jit(solution)/shard_map/ppermute | solution.py:379
  13.2 1.9 %collective-permute-done.1 = f32[2,2,8,512]{3,2,1,0:T(8,128)S(1)} collective-permute-done((f32[2,2,8,512]{3,2,1,0:T(8,128)S(1)}, f32[2,2,8,512]{3,2,1,0:T(8,128)S(1)}, u32[]{:S(2)}, u32[]{:S(2)}) %collective-permute-start.1) | collective-permute-done | bytes 65568 | tf_op jit(solution)/shard_map/ppermute | solution.py:379
  15.1 1.7 %collective-permute-start.2 = (f32[2,2,2,8,512]{4,3,2,1,0:T(8,128)S(1)}, f32[2,2,2,8,512]{4,3,2,1,0:T(8,128)S(1)}, u32[]{:S(2)}, u32[]{:S(2)}) collective-permute-start(f32[2,2,2,8,512]{4,3,2,1,0:T(8,128)S(1)} %get-tuple-element.20), channel_id=1, source_target_pairs={{0,64},{64,0},{128,192},{192,128},{1,65},{65,1},{129,193},{193,129... | collective-permute-start | bytes 393224 | tf_op jit(solution)/shard_map/ppermute | solution.py:379
  16.9 1.9 %pieces.1 = f32[8,2,8,8,128]{4,3,2,1,0:T(8,128)} custom-call(s32[1]{0:T(128)} %bitcast.14.place_ref, f32[2,64,8,512]{3,2,1,0:T(8,128)} %bitcast.37), custom_call_target="tpu_custom_call" | custom-call | tf_op jit(solution)/shard_map/pieces/pallas_call | solution.py:84
  18.7 7.3 %all-to-all-start.1 = ((f32[8,2,8,8,128]{4,3,2,1,0:T(8,128)}), f32[8,2,8,8,128]{4,3,2,1,0:T(8,128)S(1)}, u32[]{:S(2)}, u32[]{:S(2)}) async-start(f32[8,2,8,8,128]{4,3,2,1,0:T(8,128)} %pieces.1), calls=%async_computation.1 | async-start | bytes 1048576 | tf_op jit(solution)/shard_map/all_to_all | solution.py:368
  26.0 0.0 collective-permute-done.2
  26.0 0.1 fusion.2
  26.1 1.6 %collective-permute-start.3 = (f32[2,2,2,2,8,512]{5,4,3,2,1,0:T(8,128)S(1)}, f32[2,2,2,2,8,512]{5,4,3,2,1,0:T(8,128)S(1)}, u32[]{:S(2)}, u32[]{:S(2)}) collective-permute-start(f32[2,2,2,2,8,512]{5,4,3,2,1,0:T(8,128)S(1)} %get-tuple-element.18), channel_id=1, source_target_pairs={{0,16},{16,0},{32,48},{48,32},{1,17},{17,1},{33,49},{49,33},{2,18}... | collective-permute-start | bytes 786440 | tf_op jit(solution)/shard_map/ppermute | solution.py:379
  27.7 3.1 %gather_blocks.3.rest_0_ = f32[32,8,512]{2,1,0:T(8,128)} custom-call(s32[32]{0:T(128)S(1)} %copy-done.4, bf16[1024,256]{1,0:T(8,128)(2,1)S(1)} %get-tuple-element.11.left_ref, s32[32,1,512]{2,1,0:T(1,128)S(1)} %bitcast.30), custom_call_target="tpu_custom_call" | custom-call | tf_op jit(solution)/shard_map/gather_blocks/pallas_call | solution.py:160
  30.8 5.0 %gather_blocks.4.rest_0_ = f32[32,8,512]{2,1,0:T(8,128)} custom-call(s32[32]{0:T(128)S(1)} %copy-done.4, bf16[1024,256]{1,0:T(8,128)(2,1)S(1)} %get-tuple-element.11.left_ref, s32[32,1,512]{2,1,0:T(1,128)S(1)} %bitcast.31, f32[32,8,512]{2,1,0:T(8,128)} %gather_blocks.3.rest_0_), custom_call_target="tpu_custom_call", output_to_operand_aliasing={{}: (3, {})} | custom-call | tf_op jit(solution)/shard_map/gather_blocks/pallas_call | solution.py:160
  35.8 5.0 %gather_blocks.5 = f32[32,8,512]{2,1,0:T(8,128)} custom-call(s32[32]{0:T(128)S(1)} %copy-done.4, bf16[1024,256]{1,0:T(8,128)(2,1)S(1)} %get-tuple-element.11.left_ref, s32[32,1,512]{2,1,0:T(1,128)S(1)} %bitcast.32, f32[32,8,512]{2,1,0:T(8,128)} %gather_blocks.4.rest_0_), custom_call_target="tpu_custom_call", output_to_operand_aliasing={{}: (3, {})} | custom-call | tf_op jit(solution)/shard_map/gather_blocks/pallas_call | solution.py:160
  40.8 0.0 all-to-all-done.1.all_ref
  40.8 7.1 %all-to-all-start = ((f32[32,8,512]{2,1,0:T(8,128)}), f32[32,8,512]{2,1,0:T(8,128)S(1)}, u32[]{:S(2)}, u32[]{:S(2)}) async-start(f32[32,8,512]{2,1,0:T(8,128)} %gather_blocks.5), calls=%async_computation | async-start | bytes 1048576 | tf_op jit(solution)/shard_map/all_to_all | solution.py:368
  47.9 0.0 collective-permute-done.3
  48.0 0.3 collective-permute-start.4
  48.3 0.5 pick.1.own_ref
  48.9 1.6 %collective-permute-start.5 = (f32[2,8,8,128]{3,2,1,0:T(8,128)S(1)}, f32[2,8,8,128]{3,2,1,0:T(8,128)S(1)}, u32[]{:S(2)}, u32[]{:S(2)}) collective-permute-start(f32[2,8,8,128]{3,2,1,0:T(8,128)S(1)} %pick.1.own_ref), channel_id=1, source_target_pairs={{0,64},{64,0},{128,192},{192,128},{1,65},{65,1},{129,193},{193,129... | collective-permute-start | bytes 196616 | tf_op jit(solution)/shard_map/ppermute | solution.py:374
  50.5 2.1 %collective-permute-start.6 = (f32[2,8,8,128]{3,2,1,0:T(8,128)S(1)}, f32[2,8,8,128]{3,2,1,0:T(8,128)S(1)}, u32[]{:S(2)}, u32[]{:S(2)}) collective-permute-start(f32[2,8,8,128]{3,2,1,0:T(8,128)S(1)} %pick.1.own_ref), channel_id=1, source_target_pairs={{0,128},{64,192},{128,0},{192,64},{1,129},{65,193},{129,1},{193,65... | collective-permute-start | bytes 196616 | tf_op jit(solution)/shard_map/ppermute | solution.py:374
  52.6 0.1 collective-permute-start.7
  52.7 5.4 %collective-permute-done.5.one_ref = f32[2,8,8,128]{3,2,1,0:T(8,128)S(1)} collective-permute-done((f32[2,8,8,128]{3,2,1,0:T(8,128)S(1)}, f32[2,8,8,128]{3,2,1,0:T(8,128)S(1)}, u32[]{:S(2)}, u32[]{:S(2)}) %collective-permute-start.5) | collective-permute-done | bytes 65568 | tf_op jit(solution)/shard_map/ppermute | solution.py:374
  58.1 8.3 %collective-permute-done.6.two_ref = f32[2,8,8,128]{3,2,1,0:T(8,128)S(1)} collective-permute-done((f32[2,8,8,128]{3,2,1,0:T(8,128)S(1)}, f32[2,8,8,128]{3,2,1,0:T(8,128)S(1)}, u32[]{:S(2)}, u32[]{:S(2)}) %collective-permute-start.6) | collective-permute-done | bytes 65568 | tf_op jit(solution)/shard_map/ppermute | solution.py:374
  66.4 0.0 collective-permute-done.7.three_ref
  66.4 0.6 choose.1
  67.0 3.0 %collective-permute-start.10 = (f32[2,8,8,128]{3,2,1,0:T(8,128)S(1)}, f32[2,8,8,128]{3,2,1,0:T(8,128)S(1)}, u32[]{:S(2)}, u32[]{:S(2)}) collective-permute-start(f32[2,8,8,128]{3,2,1,0:T(8,128)S(1)} %choose.1), channel_id=1, source_target_pairs={{0,6},{2,4},{4,2},{6,0},{1,7},{3,5},{5,3},{7,1},{8,14},{10,12},{12... | collective-permute-start | bytes 196616 | tf_op jit(solution)/shard_map/ppermute | solution.py:374
  70.0 0.3 collective-permute-start.9
  70.4 0.3 collective-permute-start.8
  70.7 1.0 %collective-permute-done.10 = f32[2,8,8,128]{3,2,1,0:T(8,128)S(1)} collective-permute-done((f32[2,8,8,128]{3,2,1,0:T(8,128)S(1)}, f32[2,8,8,128]{3,2,1,0:T(8,128)S(1)}, u32[]{:S(2)}, u32[]{:S(2)}) %collective-permute-start.10) | collective-permute-done | bytes 65568 | tf_op jit(solution)/shard_map/ppermute | solution.py:374
  71.7 3.0 %collective-permute-done.9 = f32[2,8,8,128]{3,2,1,0:T(8,128)S(1)} collective-permute-done((f32[2,8,8,128]{3,2,1,0:T(8,128)S(1)}, f32[2,8,8,128]{3,2,1,0:T(8,128)S(1)}, u32[]{:S(2)}, u32[]{:S(2)}) %collective-permute-start.9) | collective-permute-done | bytes 65568 | tf_op jit(solution)/shard_map/ppermute | solution.py:374
  74.6 0.0 collective-permute-done.8
  74.7 0.0 collective-permute-done.4
  74.7 0.9 operands.1
  75.6 0.5 cross.1
  76.0 2.5 %collective-permute-start.13 = (f32[64,256]{1,0:T(8,128)S(1)}, f32[64,256]{1,0:T(8,128)S(1)}, u32[]{:S(2)}, u32[]{:S(2)}) collective-permute-start(f32[64,256]{1,0:T(8,128)S(1)} %cross.1), channel_id=1, source_target_pairs={{0,48},{16,32},{32,16},{48,0},{1,49},{17,33},{33,17},{49,1},{2,50}... | collective-permute-start | bytes 196616 | tf_op jit(solution)/shard_map/ppermute | solution.py:374
  78.5 0.5 collective-permute-start.12
  79.1 0.3 collective-permute-start.11
  79.4 1.1 %collective-permute-done.13 = f32[64,256]{1,0:T(8,128)S(1)} collective-permute-done((f32[64,256]{1,0:T(8,128)S(1)}, f32[64,256]{1,0:T(8,128)S(1)}, u32[]{:S(2)}, u32[]{:S(2)}) %collective-permute-start.13) | collective-permute-done | bytes 65568 | tf_op jit(solution)/shard_map/ppermute | solution.py:374
  80.4 2.7 %collective-permute-done.12 = f32[64,256]{1,0:T(8,128)S(1)} collective-permute-done((f32[64,256]{1,0:T(8,128)S(1)}, f32[64,256]{1,0:T(8,128)S(1)}, u32[]{:S(2)}, u32[]{:S(2)}) %collective-permute-start.12) | collective-permute-done | bytes 65568 | tf_op jit(solution)/shard_map/ppermute | solution.py:374
  83.2 0.0 collective-permute-done.11
  83.2 4.5 %collective-permute-start.14 = (f32[4,64,256]{2,1,0:T(8,128)S(1)}, f32[4,64,256]{2,1,0:T(8,128)S(1)}, u32[]{:S(2)}, u32[]{:S(2)}) collective-permute-start(f32[4,64,256]{2,1,0:T(8,128)S(1)} %pad_maximum_fusion.3.mine_ref), channel_id=1, source_target_pairs={{0,8},{8,0},{1,9},{9,1},{2,10},{10,2},{3,11},{11,3},{4,12},{12,4},... | collective-permute-start | bytes 786440 | tf_op jit(solution)/shard_map/ppermute | solution.py:388
  87.7 3.2 %update.1.base_ref = f32[256,512]{1,0:T(8,128)S(1)} custom-call(s32[1]{0:T(128)} %bitcast.me_ref, s32[32]{0:T(128)S(1)} %copy-done.4, bf16[256,1024]{1,0:T(8,128)(2,1)S(1)} %get-tuple-element.13.high_ref, bf16[256,1024]{1,0:T(8,128)(2,1)S(1)} %get-tuple-element.14.low_ref, f32[256,512]{1,0:T(8,128)S(1)} %get-tuple-element.15.solved_ref, f32[2,512,512]{2,1,0:T(8,128)} %panel_hbm.2), custom_call_target="tpu_custom_call" | custom-call | tf_op jit(solution)/shard_map/update/pallas_call | solution.py:259
  90.9 0.0 collective-permute-done.14.other_ref
  90.9 3.8 %tail.1.update_ref = f32[256,512]{1,0:T(8,128)S(1)} custom-call(s32[1]{0:T(128)} %bitcast.me_ref, s32[32]{0:T(128)S(1)} %copy-done.4, f32[256,512]{1,0:T(8,128)S(1)} %update.1.base_ref, f32[256,512]{1,0:T(8,128)} %get-tuple-element.16.second_hbm, f32[4,64,256]{2,1,0:T(8,128)S(1)} %pad_maximum_fusion.3.mine_ref, ...), custom_call_target="tpu_custom_call" | custom-call | tf_op jit(solution)/shard_map/tail/pallas_call | solution.py:320
  94.7 1.4 %combine.1 = f32[2,128,512]{2,1,0:T(8,128)} custom-call(s32[1]{0:T(128)} %bitcast.me_ref, s32[32]{0:T(128)S(1)} %copy-done.4, f32[32,8,512]{2,1,0:T(8,128)S(1)} %all-to-all-done.current_ref, f32[256,512]{1,0:T(8,128)S(1)} %tail.1.update_ref), custom_call_target="tpu_custom_call" | custom-call | tf_op jit(solution)/shard_map/combine/pallas_call | solution.py:353
  (14 shorter events, 0.1 us)
Async XLA Ops:
  0.0 1.6 %copy-start = (f32[2,512,512]{2,1,0:T(8,128)S(1)}, f32[2,512,512]{2,1,0:T(8,128)}, u32[]{:S(2)}) copy-start(f32[2,512,512]{2,1,0:T(8,128)} %inverse_ref.2) | copy-start | bytes 6291460
  1.6 0.8 copy-start.2
  5.2 5.2 %collective-permute-start = (f32[2,8,512]{2,1,0:T(8,128)S(1)}, f32[2,8,512]{2,1,0:T(8,128)S(1)}, u32[]{:S(2)}, u32[]{:S(2)}) collective-permute-start(f32[2,8,512]{2,1,0:T(8,128)S(1)} %get-tuple-element.12), channel_id=1, source_target_pairs={{0,128},{64,192},{128,0},{192,64},{1,129},{65,193},{129,1},{193,65... | collective-permute-start | bytes 98312 | tf_op jit(solution)/shard_map/ppermute | solution.py:379
  10.4 4.7 %collective-permute-start.1 = (f32[2,2,8,512]{3,2,1,0:T(8,128)S(1)}, f32[2,2,8,512]{3,2,1,0:T(8,128)S(1)}, u32[]{:S(2)}, u32[]{:S(2)}) collective-permute-start(f32[2,2,8,512]{3,2,1,0:T(8,128)S(1)} %get-tuple-element.22), channel_id=1, source_target_pairs={{0,32},{16,48},{32,0},{48,16},{1,33},{17,49},{33,1},{49,17},{2,34}... | collective-permute-start | bytes 196616 | tf_op jit(solution)/shard_map/ppermute | solution.py:379
  15.1 10.9 %collective-permute-start.2 = (f32[2,2,2,8,512]{4,3,2,1,0:T(8,128)S(1)}, f32[2,2,2,8,512]{4,3,2,1,0:T(8,128)S(1)}, u32[]{:S(2)}, u32[]{:S(2)}) collective-permute-start(f32[2,2,2,8,512]{4,3,2,1,0:T(8,128)S(1)} %get-tuple-element.20), channel_id=1, source_target_pairs={{0,64},{64,0},{128,192},{192,128},{1,65},{65,1},{129,193},{193,129... | collective-permute-start | bytes 393224 | tf_op jit(solution)/shard_map/ppermute | solution.py:379
  16.9 10.8 %copy-start.3 = (s32[16384]{0:T(1024)S(1)}, s32[16384]{0:T(1024)}, u32[]{:S(2)}) copy-start(s32[16384]{0:T(1024)} %param.8) | copy-start | bytes 196612
  16.9 10.8 %copy-start.4 = (s32[32]{0:T(128)S(1)}, s32[32]{0:T(128)}, u32[]{:S(2)}) copy-start(s32[32]{0:T(128)} %owners_ref.15) | copy-start | bytes 388
  18.7 22.0 %all-to-all-start.1 = ((f32[8,2,8,8,128]{4,3,2,1,0:T(8,128)}), f32[8,2,8,8,128]{4,3,2,1,0:T(8,128)S(1)}, u32[]{:S(2)}, u32[]{:S(2)}) async-start(f32[8,2,8,8,128]{4,3,2,1,0:T(8,128)} %pieces.1), calls=%async_computation.1 | async-start | bytes 1048576 | tf_op jit(solution)/shard_map/all_to_all | solution.py:368
  26.1 21.9 %collective-permute-start.3 = (f32[2,2,2,2,8,512]{5,4,3,2,1,0:T(8,128)S(1)}, f32[2,2,2,2,8,512]{5,4,3,2,1,0:T(8,128)S(1)}, u32[]{:S(2)}, u32[]{:S(2)}) collective-permute-start(f32[2,2,2,2,8,512]{5,4,3,2,1,0:T(8,128)S(1)} %get-tuple-element.18), channel_id=1, source_target_pairs={{0,16},{16,0},{32,48},{48,32},{1,17},{17,1},{33,49},{49,33},{2,18}... | collective-permute-start | bytes 786440 | tf_op jit(solution)/shard_map/ppermute | solution.py:379
  40.8 53.9 %all-to-all-start = ((f32[32,8,512]{2,1,0:T(8,128)}), f32[32,8,512]{2,1,0:T(8,128)S(1)}, u32[]{:S(2)}, u32[]{:S(2)}) async-start(f32[32,8,512]{2,1,0:T(8,128)} %gather_blocks.5), calls=%async_computation | async-start | bytes 1048576 | tf_op jit(solution)/shard_map/all_to_all | solution.py:368
  48.0 26.7 %collective-permute-start.4 = (f32[2,2,2,2,2,8,512]{6,5,4,3,2,1,0:T(8,128)S(1)}, f32[2,2,2,2,2,8,512]{6,5,4,3,2,1,0:T(8,128)S(1)}, u32[]{:S(2)}, u32[]{:S(2)}) collective-permute-start(f32[2,2,2,2,2,8,512]{6,5,4,3,2,1,0:T(8,128)S(1)} %pad_maximum_fusion), channel_id=1, source_target_pairs={{0,8},{8,0},{1,9},{9,1},{2,10},{10,2},{3,11},{11,3},{4,12},{12,4},... | collective-permute-start | bytes 1572872 | tf_op jit(solution)/shard_map/ppermute | solution.py:388
  48.9 9.2 %collective-permute-start.5 = (f32[2,8,8,128]{3,2,1,0:T(8,128)S(1)}, f32[2,8,8,128]{3,2,1,0:T(8,128)S(1)}, u32[]{:S(2)}, u32[]{:S(2)}) collective-permute-start(f32[2,8,8,128]{3,2,1,0:T(8,128)S(1)} %pick.1.own_ref), channel_id=1, source_target_pairs={{0,64},{64,0},{128,192},{192,128},{1,65},{65,1},{129,193},{193,129... | collective-permute-start | bytes 196616 | tf_op jit(solution)/shard_map/ppermute | solution.py:374
  50.5 15.9 %collective-permute-start.6 = (f32[2,8,8,128]{3,2,1,0:T(8,128)S(1)}, f32[2,8,8,128]{3,2,1,0:T(8,128)S(1)}, u32[]{:S(2)}, u32[]{:S(2)}) collective-permute-start(f32[2,8,8,128]{3,2,1,0:T(8,128)S(1)} %pick.1.own_ref), channel_id=1, source_target_pairs={{0,128},{64,192},{128,0},{192,64},{1,129},{65,193},{129,1},{193,65... | collective-permute-start | bytes 196616 | tf_op jit(solution)/shard_map/ppermute | solution.py:374
  52.6 13.8 %collective-permute-start.7 = (f32[2,8,8,128]{3,2,1,0:T(8,128)S(1)}, f32[2,8,8,128]{3,2,1,0:T(8,128)S(1)}, u32[]{:S(2)}, u32[]{:S(2)}) collective-permute-start(f32[2,8,8,128]{3,2,1,0:T(8,128)S(1)} %pick.1.own_ref), channel_id=1, source_target_pairs={{0,192},{64,128},{128,64},{192,0},{1,193},{65,129},{129,65},{193,1... | collective-permute-start | bytes 196616 | tf_op jit(solution)/shard_map/ppermute | solution.py:374
  67.0 4.7 %collective-permute-start.10 = (f32[2,8,8,128]{3,2,1,0:T(8,128)S(1)}, f32[2,8,8,128]{3,2,1,0:T(8,128)S(1)}, u32[]{:S(2)}, u32[]{:S(2)}) collective-permute-start(f32[2,8,8,128]{3,2,1,0:T(8,128)S(1)} %choose.1), channel_id=1, source_target_pairs={{0,6},{2,4},{4,2},{6,0},{1,7},{3,5},{5,3},{7,1},{8,14},{10,12},{12... | collective-permute-start | bytes 196616 | tf_op jit(solution)/shard_map/ppermute | solution.py:374
  70.0 4.6 %collective-permute-start.9 = (f32[2,8,8,128]{3,2,1,0:T(8,128)S(1)}, f32[2,8,8,128]{3,2,1,0:T(8,128)S(1)}, u32[]{:S(2)}, u32[]{:S(2)}) collective-permute-start(f32[2,8,8,128]{3,2,1,0:T(8,128)S(1)} %choose.1), channel_id=1, source_target_pairs={{0,4},{2,6},{4,0},{6,2},{1,5},{3,7},{5,1},{7,3},{8,12},{10,14},{12... | collective-permute-start | bytes 196616 | tf_op jit(solution)/shard_map/ppermute | solution.py:374
  70.4 4.3 %collective-permute-start.8 = (f32[2,8,8,128]{3,2,1,0:T(8,128)S(1)}, f32[2,8,8,128]{3,2,1,0:T(8,128)S(1)}, u32[]{:S(2)}, u32[]{:S(2)}) collective-permute-start(f32[2,8,8,128]{3,2,1,0:T(8,128)S(1)} %choose.1), channel_id=1, source_target_pairs={{0,2},{2,0},{4,6},{6,4},{1,3},{3,1},{5,7},{7,5},{8,10},{10,8},{12,... | collective-permute-start | bytes 196616 | tf_op jit(solution)/shard_map/ppermute | solution.py:374
  76.0 4.4 %collective-permute-start.13 = (f32[64,256]{1,0:T(8,128)S(1)}, f32[64,256]{1,0:T(8,128)S(1)}, u32[]{:S(2)}, u32[]{:S(2)}) collective-permute-start(f32[64,256]{1,0:T(8,128)S(1)} %cross.1), channel_id=1, source_target_pairs={{0,48},{16,32},{32,16},{48,0},{1,49},{17,33},{33,17},{49,1},{2,50}... | collective-permute-start | bytes 196616 | tf_op jit(solution)/shard_map/ppermute | solution.py:374
  78.5 4.6 %collective-permute-start.12 = (f32[64,256]{1,0:T(8,128)S(1)}, f32[64,256]{1,0:T(8,128)S(1)}, u32[]{:S(2)}, u32[]{:S(2)}) collective-permute-start(f32[64,256]{1,0:T(8,128)S(1)} %cross.1), channel_id=1, source_target_pairs={{0,32},{16,48},{32,0},{48,16},{1,33},{17,49},{33,1},{49,17},{2,34}... | collective-permute-start | bytes 196616 | tf_op jit(solution)/shard_map/ppermute | solution.py:374
  79.1 4.1 %collective-permute-start.11 = (f32[64,256]{1,0:T(8,128)S(1)}, f32[64,256]{1,0:T(8,128)S(1)}, u32[]{:S(2)}, u32[]{:S(2)}) collective-permute-start(f32[64,256]{1,0:T(8,128)S(1)} %cross.1), channel_id=1, source_target_pairs={{0,16},{16,0},{32,48},{48,32},{1,17},{17,1},{33,49},{49,33},{2,18}... | collective-permute-start | bytes 196616 | tf_op jit(solution)/shard_map/ppermute | solution.py:374
  83.2 7.7 %collective-permute-start.14 = (f32[4,64,256]{2,1,0:T(8,128)S(1)}, f32[4,64,256]{2,1,0:T(8,128)S(1)}, u32[]{:S(2)}, u32[]{:S(2)}) collective-permute-start(f32[4,64,256]{2,1,0:T(8,128)S(1)} %pad_maximum_fusion.3.mine_ref), channel_id=1, source_target_pairs={{0,8},{8,0},{1,9},{9,1},{2,10},{10,2},{3,11},{11,3},{4,12},{12,4},... | collective-permute-start | bytes 786440 | tf_op jit(solution)/shard_map/ppermute | solution.py:388
  87.7 3.3 %copy-start.1 = (f32[2,512,512]{2,1,0:T(8,128)S(1)}, f32[2,512,512]{2,1,0:T(8,128)}, u32[]{:S(2)}) copy-start(f32[2,512,512]{2,1,0:T(8,128)} %inverse_ref.3) | copy-start | bytes 6291460
